TPU v7x, 256 devices: a whole 4x4x8 slice. The times are simulated.
256 devices in a mesh: blk: 128 (over z, y_lo, x, core), dp: 2 (over y_hi).
Axes of the slice: x: 4, y: 4 (y_hi: 2, y_lo: 2; y = y_hi * 2 + y_lo), z: 8, core: 2. Of those that a mesh axis runs over, the one named last changes fastest.
Arguments:
- tokens: bfloat16 [49152, 2048], P(('blk', 'dp')), may hold values from -6 to 6
- cotangent: bfloat16 [49152, 2048], P(('blk', 'dp')), may hold values from -0.59765625 to 0.59765625
- gate_probs: bfloat16 [49152, 3], P(('blk', 'dp')), may hold values from 0.099609375 to 1
- slot_rows: int32 [384, 128], P('blk'), may hold values from 0 to 384, as said below
- w_gate: bfloat16 [128, 2048, 768], P('blk', None, 'dp'), may hold values from -0.125 to 0.125
- w_up: bfloat16 [128, 2048, 768], P('blk', None, 'dp'), may hold values from -0.125 to 0.125
- w_down: bfloat16 [128, 768, 2048], P('blk', 'dp'), may hold values from -0.21875 to 0.21875
Outputs:
- mixed: bfloat16 [49152, 2048], P(('blk', 'dp'))
- input_grad: bfloat16 [49152, 2048], P(('blk', 'dp'))
- gate_grad: float32 [49152, 3], P(('blk', 'dp'))
- w_gate_grad: bfloat16 [128, 2048, 768], P('blk', None, 'dp')
- w_up_grad: bfloat16 [128, 2048, 768], P('blk', None, 'dp')
- w_down_grad: bfloat16 [128, 768, 2048], P('blk', 'dp')
Inputs may be any that keep to these rules, and one draw needn't show every extreme that they name: `slot_rows`: entries below 384 in a row are distinct and stand before the entries equal to 384; every row names at least 16 tokens, and some row names 128.
All inputs are finite; a program needn't handle non-finite values.
Results may differ from a plain program's by a relative error of at most 0.0075.
Values may be sent and summed in bfloat16 or wider, within the bound.
A program may use at most 128 MiB of HBM per device.

v0:
```python
import jax
import jax.numpy as jnp
from jax import lax
from jax.sharding import PartitionSpec as P


def shifted(value, axis, steps):
    count = lax.axis_size(axis)
    pairs = [(source, (source + steps) % count) for source in range(count)]
    return lax.ppermute(value, axis, pairs)


def shortened(x):
    return jax.tree.map(lambda a: a.astype(jnp.bfloat16) if a.dtype == jnp.float32 else a, x)


def expert_step(slab, rows_x, rows_dy, rows_gate):
    w_gate_s, w_up_s, w_down_s = slab
    gate_rows = rows_gate.astype(jnp.float32)
    pre_gate = jnp.dot(rows_x, w_gate_s, preferred_element_type=jnp.float32)
    pre_up = jnp.dot(rows_x, w_up_s, preferred_element_type=jnp.float32)
    sigmoid_gate = jax.nn.sigmoid(pre_gate)
    active = pre_gate * sigmoid_gate
    hidden = (active * pre_up).astype(jnp.bfloat16)
    expert_out = jnp.dot(hidden, w_down_s, preferred_element_type=jnp.float32)
    weighted = gate_rows[:, None] * expert_out
    cotan_rows = rows_dy.astype(jnp.float32)
    gate_grad = jnp.sum(cotan_rows * expert_out, axis=1)
    out_grad = (gate_rows[:, None] * cotan_rows).astype(jnp.bfloat16)
    hidden_grad = jnp.einsum("cd,hd->ch", out_grad, w_down_s, preferred_element_type=jnp.float32)
    pre_gate_grad = (
        hidden_grad * pre_up * sigmoid_gate * (1.0 + pre_gate * (1.0 - sigmoid_gate))
    ).astype(jnp.bfloat16)
    pre_up_grad = (hidden_grad * active).astype(jnp.bfloat16)
    input_grad = jnp.einsum(
        "ch,dh->cd", pre_gate_grad, w_gate_s, preferred_element_type=jnp.float32
    )
    input_grad = input_grad + jnp.einsum(
        "ch,dh->cd", pre_up_grad, w_up_s, preferred_element_type=jnp.float32
    )
    part_gate = jnp.einsum(
        "cd,ch->dh", rows_x, pre_gate_grad, preferred_element_type=jnp.float32
    ).astype(jnp.bfloat16)
    part_up = jnp.einsum(
        "cd,ch->dh", rows_x, pre_up_grad, preferred_element_type=jnp.float32
    ).astype(jnp.bfloat16)
    part_down = jnp.einsum(
        "ch,cd->hd", hidden, out_grad, preferred_element_type=jnp.float32
    ).astype(jnp.bfloat16)
    return ((weighted, input_grad, gate_grad), (part_gate, part_up, part_down))


def add_partials(totals, partials):
    return tuple((first + second.astype(jnp.float32) for first, second in zip(totals, partials)))


def on_device(tokens, cotangent, gate_probs, slot_rows, w_gate, w_up, w_down):
    group_x, group_dy, group_gate = (
        lax.all_gather(tokens, "dp", axis=0, tiled=True),
        lax.all_gather(cotangent, "dp", axis=0, tiled=True),
        lax.all_gather(gate_probs, "dp", axis=0, tiled=True),
    )
    model_width = tokens.shape[1]
    cycle_steps = slot_rows.shape[0]
    group_size = group_x.shape[0]
    padded_x = jnp.concatenate([group_x, jnp.zeros((1, model_width), group_x.dtype)], axis=0)
    padded_dy = jnp.concatenate([group_dy, jnp.zeros((1, model_width), group_dy.dtype)], axis=0)
    padded_gate = jnp.concatenate(
        [group_gate, jnp.zeros((1, cycle_steps), group_gate.dtype)], axis=0
    )
    own_slab = (w_gate[0], w_up[0], w_down[0])
    mixed_acc = jnp.zeros((group_size + 1, model_width), jnp.float32)
    input_acc = jnp.zeros((group_size + 1, model_width), jnp.float32)
    gate_acc = jnp.zeros((group_size + 1, cycle_steps), jnp.float32)
    totals = (
        jnp.zeros(w_gate.shape[1:], jnp.float32),
        jnp.zeros(w_up.shape[1:], jnp.float32),
        jnp.zeros(w_down.shape[1:], jnp.float32),
    )
    fetched = [own_slab]
    current = own_slab
    for cycle_step in range(1, cycle_steps):
        current = shifted((current[0], current[1], current[2]), "blk", 1)
        fetched.append(current)
    outgoing = []
    for cycle_step in range(cycle_steps):
        list_rows = slot_rows[cycle_step]
        list_rows, rows_x, rows_dy, rows_gate = (
            list_rows,
            padded_x[list_rows],
            padded_dy[list_rows],
            padded_gate[list_rows, cycle_step],
        )
        results, partials = expert_step(fetched[cycle_step], rows_x, rows_dy, rows_gate)
        mixed_acc = mixed_acc.at[list_rows].add(results[0])
        input_acc = input_acc.at[list_rows].add(results[1])
        gate_acc = gate_acc.at[list_rows, cycle_step].add(results[2])
        if cycle_step == 0:
            totals = add_partials(totals, partials)
        else:
            outgoing.append(partials)
    for cycle_step in range(1, cycle_steps):
        arrived = shifted(shortened(outgoing[cycle_step - 1]), "blk", -cycle_step)
        totals = add_partials(totals, arrived)
    summed = (
        lax.psum_scatter(mixed_acc[:group_size], "dp", scatter_dimension=0, tiled=True),
        lax.psum_scatter(input_acc[:group_size], "dp", scatter_dimension=0, tiled=True),
        lax.psum_scatter(gate_acc[:group_size], "dp", scatter_dimension=0, tiled=True),
    )
    mixed = summed[0].astype(jnp.bfloat16)
    input_grad = summed[1].astype(jnp.bfloat16)
    gate_grad = summed[2]
    return (
        mixed,
        input_grad,
        gate_grad,
        totals[0].astype(jnp.bfloat16)[None],
        totals[1].astype(jnp.bfloat16)[None],
        totals[2].astype(jnp.bfloat16)[None],
    )


def solution(mesh):
    in_specs = (
        P(("blk", "dp"), None),
        P(("blk", "dp"), None),
        P(("blk", "dp"), None),
        P("blk", None),
        P("blk", None, "dp"),
        P("blk", None, "dp"),
        P("blk", "dp", None),
    )
    out_specs = (
        P(("blk", "dp"), None),
        P(("blk", "dp"), None),
        P(("blk", "dp"), None),
        P("blk", None, "dp"),
        P("blk", None, "dp"),
        P("blk", "dp", None),
    )
    return jax.shard_map(
        on_device, mesh=mesh, in_specs=in_specs, out_specs=out_specs, check_vma=False
    )
```

profile of v0, /device:TPU:1, one launch (start us, length us, event | category | flops | bytes accessed | tf_op | source)
XLA Modules:
  0.0 484.0 jit_solution(8801127587306219568)
XLA Ops:
  8.7 2.7 collective-permute-start.2
  11.5 1.5 collective-permute-start
  13.0 4.9 %all-gather = bf16[2,192,3]{1,2,0:T(4,128)(2,1)S(1)} all-gather(bf16[1,192,3]{1,2,0:T(4,128)(2,1)S(1)} %bitcast.104), channel_id=1, replica_groups=mesh['blk'=128,'dp'=2] {'dp'}, dimensions={0}, use_global_device_ids=true | all-gather | bytes 3456 | tf_op jit(solution)/shard_map/all_gather | solution.py:61
  18.2 1.5 gather_fusion
  19.7 1.5 gather_fusion.2
  21.3 1.5 gather_fusion.4
  22.9 62.3 %all-gather.4.cloned.1.call-done = bf16[384,2048]{1,0:T(8,128)(2,1)} async-done(((bf16[192,2048]{1,0:T(8,128)(2,1)}), bf16[384,2048]{1,0:T(8,128)(2,1)}) %all-gather.4.cloned.1.call-update) | async-done | bytes 1572880 | tf_op jit(solution)/shard_map/all_gather | solution.py:59
  85.2 1.6 concatenate.23
  86.8 1.7 gather_fusion.1
  88.5 31.7 %all-gather.6.cloned.1.call-done = bf16[384,2048]{1,0:T(8,128)(2,1)} async-done(((bf16[192,2048]{1,0:T(8,128)(2,1)}), bf16[384,2048]{1,0:T(8,128)(2,1)}) %all-gather.6.cloned.1.call-update) | async-done | bytes 1572880 | tf_op jit(solution)/shard_map/all_gather | solution.py:60
  120.2 1.6 concatenate.26
  121.8 1.7 gather_fusion.6
  123.5 1.7 gather_fusion.7
  125.2 1.8 gather_fusion.3
  127.0 1.9 collective-permute-start.5
  129.0 2.0 fusion.45
  131.0 1.9 fusion.49
  133.0 2.1 multiply_convert_fusion.4
  135.1 2.1 fusion.47
  137.2 3.1 convolution_add_fusion.2
  140.3 2.0 collective-permute-start.3
  142.3 2.0 fusion.25
  144.3 1.8 fusion.51
  146.2 2.6 multiply_convert_fusion.3
  148.7 3.0 fusion.53
  151.8 1.7 gather_fusion.8
  153.5 1.7 gather_fusion.5
  155.2 3.6 scatter_custom_fusion.3
  158.9 3.3 convolution_add_fusion.1
  162.2 4.0 scatter_fusion
  166.2 2.9 fusion.8
  169.1 6.9 %scatter_fusion.2 = f32[385,3]{0,1:T(4,128)S(1)} fusion(f32[385,3]{0,1:T(4,128)S(1)} %broadcast_in_dim.8, s32[128]{0:T(128)S(1)} %get-tuple-element.21, f32[128]{0:T(128)S(1)} %get-tuple-element.25), kind=kCustom, calls=%fused_computation.15 | custom fusion | flops 128 | bytes 2560 | tf_op jit(solution)/shard_map/scatter-add | solution.py:97
  176.1 2.9 fusion.10
  179.0 7.0 %scatter_fusion.3 = f32[385,3]{0,1:T(4,128)S(1)} fusion(f32[385,3]{0,1:T(4,128)S(1)} %scatter_fusion.2, s32[128]{0:T(128)S(1)} %get-tuple-element.23, f32[128]{0:T(128)S(1)} %get-tuple-element.27), kind=kCustom, calls=%fused_computation.16 | custom fusion | flops 128 | bytes 2560 | tf_op jit(solution)/shard_map/scatter-add | solution.py:97
  186.0 2.1 fusion.52
  188.1 2.1 fusion.22
  190.2 2.6 multiply_convert_fusion.1
  192.8 2.8 fusion.12
  195.6 6.9 %scatter_fusion.4 = f32[385,3]{0,1:T(4,128)S(1)} fusion(f32[385,3]{0,1:T(4,128)S(1)} %scatter_fusion.3, s32[128]{0:T(128)S(1)} %get-tuple-element.6, f32[128]{0:T(128)S(1)} %get-tuple-element.29), kind=kCustom, calls=%fused_computation.17 | custom fusion | flops 128 | bytes 2560 | tf_op jit(solution)/shard_map/scatter-add | solution.py:97
  203.5 2.1 fusion.54
  205.6 3.0 convolution_add_fusion
  208.6 4.2 scatter_fusion.1
  212.8 2.0 slice.49
  214.9 3.7 scatter_custom_fusion
  218.7 4.1 scatter_custom_fusion.1
  222.8 4.1 scatter_custom_fusion.2
  227.0 1.9 slice.48
  230.9 1.7 convolution_convert_fusion.7
  232.7 4.7 collective-permute-start.6
  238.3 1.7 convolution_convert_fusion.6
  241.2 1.8 convolution_convert_fusion.4
  243.9 1.8 convolution_convert_fusion.3
  245.6 15.2 %collective-permute-done.10 = bf16[384,2048]{1,0:T(8,128)(2,1)S(1)} collective-permute-done((bf16[384,2048]{1,0:T(8,128)(2,1)S(1)}, bf16[384,2048]{1,0:T(8,128)(2,1)S(1)}, u32[]{:S(2)}, u32[]{:S(2)}) %collective-permute-start.10) | collective-permute-done | bytes 1572896 | tf_op jit(solution)/shard_map/ppermute | solution.py:10
  262.0 12.8 %collective-permute-start.9 = (bf16[2048,384]{1,0:T(8,128)(2,1)}, bf16[2048,384]{1,0:T(8,128)(2,1)}, u32[]{:S(2)}, u32[]{:S(2)}) collective-permute-start(bf16[2048,384]{1,0:T(8,128)(2,1)} %convolution_convert_fusion.3), channel_id=1, source_target_pairs={{0,252},{2,254},{4,0},{6,2},{8,4},{10,6},{12,8},{14,10},{16,12},{1... | collective-permute-start | bytes 4718600 | tf_op jit(solution)/shard_map/ppermute | solution.py:10
  274.8 1.6 copy.19
  276.4 3.8 fusion.2
  280.2 14.0 %collective-permute-done.6 = bf16[2048,384]{1,0:T(8,128)(2,1)} collective-permute-done((bf16[2048,384]{1,0:T(8,128)(2,1)}, bf16[2048,384]{1,0:T(8,128)(2,1)}, u32[]{:S(2)}, u32[]{:S(2)}) %collective-permute-start.6) | collective-permute-done | bytes 1572896 | tf_op jit(solution)/shard_map/ppermute | solution.py:10
  294.2 14.1 %collective-permute-done.7 = bf16[2048,384]{1,0:T(8,128)(2,1)} collective-permute-done((bf16[2048,384]{1,0:T(8,128)(2,1)}, bf16[2048,384]{1,0:T(8,128)(2,1)}, u32[]{:S(2)}, u32[]{:S(2)}) %collective-permute-start.7) | collective-permute-done | bytes 1572896 | tf_op jit(solution)/shard_map/ppermute | solution.py:10
  308.3 3.7 fusion
  312.1 56.5 %collective-permute-done.8 = bf16[2048,384]{1,0:T(8,128)(2,1)} collective-permute-done((bf16[2048,384]{1,0:T(8,128)(2,1)}, bf16[2048,384]{1,0:T(8,128)(2,1)}, u32[]{:S(2)}, u32[]{:S(2)}) %collective-permute-start.8) | collective-permute-done | bytes 1572896 | tf_op jit(solution)/shard_map/ppermute | solution.py:10
  368.6 3.7 fusion.1
  372.3 2.4 convert_element_type.154
  374.7 100.2 %reduce-scatter.6.cloned.1.call-done = f32[192,2048]{1,0:T(8,128)} async-done(((f32[384,2048]{1,0:T(8,128)}), f32[192,2048]{1,0:T(8,128)}) %reduce-scatter.6.cloned.1.call-update) | async-done | bytes 1572880 | tf_op jit(solution)/shard_map/reduce_scatter | solution.py:106
  474.8 2.4 convert_element_type.141
  (94 shorter events, 9.2 us)
Async XLA Ops:
  7.2 5.8 %copy-start.24 = (bf16[192,3]{0,1:T(4,128)(2,1)S(1)}, bf16[192,3]{0,1:T(4,128)(2,1)}, u32[]{:S(2)}) copy-start(bf16[192,3]{0,1:T(4,128)(2,1)} %param.9) | copy-start | bytes 3460
  7.2 11.0 %copy-start.25 = (s32[3,128]{1,0:T(4,128)S(1)}, s32[3,128]{1,0:T(4,128)}, u32[]{:S(2)}) copy-start(s32[3,128]{1,0:T(4,128)} %param.10) | copy-start | bytes 4612
  7.2 78.0 %all-gather.4.cloned.1.call-start = ((), (), s32[]{:S(2)}) async-start(), calls=%async_computation.3 | async-start | bytes 2359296 | tf_op jit(solution)/shard_map/all_gather | solution.py:59
  7.9 112.3 %all-gather.6.cloned.1.call-start = ((), (), s32[]{:S(2)}) async-start(), calls=%async_computation.5 | async-start | bytes 2359296 | tf_op jit(solution)/shard_map/all_gather | solution.py:60
  8.7 266.1 %reduce-scatter.10.cloned.1.call-start = ((), (), s32[]{:S(2)}) async-start(), calls=%async_computation.7 | async-start | bytes 294912
  8.7 118.3 %collective-permute-start.2 = (bf16[384,2048]{1,0:T(8,128)(2,1)}, bf16[384,2048]{1,0:T(8,128)(2,1)}, u32[]{:S(2)}, u32[]{:S(2)}) collective-permute-start(bf16[384,2048]{1,0:T(8,128)(2,1)} %bitcast.7), channel_id=1, source_target_pairs={{0,2},{2,4},{4,6},{6,8},{8,10},{10,12},{12,14},{14,16},{16,18},{18... | collective-permute-start | bytes 4718600 | tf_op jit(solution)/shard_map/ppermute | solution.py:10
  11.4 117.5 %collective-permute-start.1 = (bf16[2048,384]{1,0:T(8,128)(2,1)}, bf16[2048,384]{1,0:T(8,128)(2,1)}, u32[]{:S(2)}, u32[]{:S(2)}) collective-permute-start(bf16[2048,384]{1,0:T(8,128)(2,1)} %bitcast.6), channel_id=1, source_target_pairs={{0,2},{2,4},{4,6},{6,8},{8,10},{10,12},{12,14},{14,16},{16,18},{18... | collective-permute-start | bytes 4718600 | tf_op jit(solution)/shard_map/ppermute | solution.py:10
  11.5 128.8 %collective-permute-start = (bf16[2048,384]{1,0:T(8,128)(2,1)}, bf16[2048,384]{1,0:T(8,128)(2,1)}, u32[]{:S(2)}, u32[]{:S(2)}) collective-permute-start(bf16[2048,384]{1,0:T(8,128)(2,1)} %bitcast.5), channel_id=1, source_target_pairs={{0,2},{2,4},{4,6},{6,8},{8,10},{10,12},{12,14},{14,16},{16,18},{18... | collective-permute-start | bytes 4718600 | tf_op jit(solution)/shard_map/ppermute | solution.py:10
  127.0 4.0 copy-start
  127.0 61.1 %collective-permute-start.5 = (bf16[384,2048]{1,0:T(8,128)(2,1)}, bf16[384,2048]{1,0:T(8,128)(2,1)}, u32[]{:S(2)}, u32[]{:S(2)}) collective-permute-start(bf16[384,2048]{1,0:T(8,128)(2,1)} %collective-permute-done.2), channel_id=1, source_target_pairs={{0,2},{2,4},{4,6},{6,8},{8,10},{10,12},{12,14},{14,16},{16,18},{18... | collective-permute-start | bytes 4718600 | tf_op jit(solution)/shard_map/ppermute | solution.py:10
  128.9 57.1 %collective-permute-start.4 = (bf16[2048,384]{1,0:T(8,128)(2,1)}, bf16[2048,384]{1,0:T(8,128)(2,1)}, u32[]{:S(2)}, u32[]{:S(2)}) collective-permute-start(bf16[2048,384]{1,0:T(8,128)(2,1)} %collective-permute-done.1), channel_id=1, source_target_pairs={{0,2},{2,4},{4,6},{6,8},{8,10},{10,12},{12,14},{14,16},{16,18},{18... | collective-permute-start | bytes 4718600 | tf_op jit(solution)/shard_map/ppermute | solution.py:10
  131.0 2.0 copy-start.10
  135.1 5.2 %copy-start.20 = (bf16[128,384]{1,0:T(8,128)(2,1)}, bf16[128,384]{1,0:T(8,128)(2,1)S(1)}, u32[]{:S(2)}) copy-start(bf16[128,384]{1,0:T(8,128)(2,1)S(1)} %get-tuple-element.18) | copy-start | bytes 294916
  135.1 5.2 %copy-start.22 = (bf16[128,384]{1,0:T(8,128)(2,1)}, bf16[128,384]{1,0:T(8,128)(2,1)S(1)}, u32[]{:S(2)}) copy-start(bf16[128,384]{1,0:T(8,128)(2,1)S(1)} %get-tuple-element.19) | copy-start | bytes 294916
  137.2 5.1 %copy-start.2 = (bf16[128,2048]{1,0:T(8,128)(2,1)S(1)}, bf16[128,2048]{1,0:T(8,128)(2,1)}, u32[]{:S(2)}) copy-start(bf16[128,2048]{1,0:T(8,128)(2,1)} %gather_fusion.7) | copy-start | bytes 1572868
  140.3 4.1 copy-start.6
  140.3 49.9 %collective-permute-start.3 = (bf16[2048,384]{1,0:T(8,128)(2,1)}, bf16[2048,384]{1,0:T(8,128)(2,1)}, u32[]{:S(2)}, u32[]{:S(2)}) collective-permute-start(bf16[2048,384]{1,0:T(8,128)(2,1)} %collective-permute-done), channel_id=1, source_target_pairs={{0,2},{2,4},{4,6},{6,8},{8,10},{10,12},{12,14},{14,16},{16,18},{18... | collective-permute-start | bytes 4718600 | tf_op jit(solution)/shard_map/ppermute | solution.py:10
  148.7 4.8 copy-start.13
  155.2 3.6 copy-start.15
  186.0 2.1 copy-start.4
  188.1 2.1 copy-start.8
  203.4 168.8 %reduce-scatter.8.cloned.1.call-start = ((), (), s32[]{:S(2)}) async-start(), calls=%async_computation.6 | async-start | bytes 4718592 | tf_op jit(solution)/shard_map/reduce_scatter | solution.py:107
  203.5 2.1 copy-start.18
  214.9 260.0 %reduce-scatter.6.cloned.1.call-start = ((), (), s32[]{:S(2)}) async-start(), calls=%async_computation.4 | async-start | bytes 4718592 | tf_op jit(solution)/shard_map/reduce_scatter | solution.py:106
  228.9 1.0 copy-start.3
  229.9 1.0 copy-start.7
  229.9 1.0 copy-start.16
  230.5 6.8 %copy-start.5 = (bf16[128,2048]{1,0:T(8,128)(2,1)S(1)}, bf16[128,2048]{1,0:T(8,128)(2,1)}, u32[]{:S(2)}) copy-start(bf16[128,2048]{1,0:T(8,128)(2,1)} %gather_fusion.8) | copy-start | bytes 1572868
  230.6 30.3 %collective-permute-start.10 = (bf16[384,2048]{1,0:T(8,128)(2,1)S(1)}, bf16[384,2048]{1,0:T(8,128)(2,1)S(1)}, u32[]{:S(2)}, u32[]{:S(2)}) collective-permute-start(bf16[384,2048]{1,0:T(8,128)(2,1)S(1)} %convolution_convert_fusion.1), channel_id=1, source_target_pairs={{0,254},{2,0},{4,2},{6,4},{8,6},{10,8},{12,10},{14,12},{16,14},{18... | collective-permute-start | bytes 4718600 | tf_op jit(solution)/shard_map/ppermute | solution.py:10
  232.7 5.7 %copy-start.9 = (bf16[128,2048]{1,0:T(8,128)(2,1)S(1)}, bf16[128,2048]{1,0:T(8,128)(2,1)}, u32[]{:S(2)}) copy-start(bf16[128,2048]{1,0:T(8,128)(2,1)} %gather_fusion.5) | copy-start | bytes 1572868
  232.7 5.7 %copy-start.19 = (bf16[128,384]{1,0:T(8,128)(2,1)S(1)}, bf16[128,384]{1,0:T(8,128)(2,1)}, u32[]{:S(2)}) copy-start(bf16[128,384]{1,0:T(8,128)(2,1)} %get-tuple-element.12) | copy-start | bytes 294916
  232.7 61.5 %collective-permute-start.6 = (bf16[2048,384]{1,0:T(8,128)(2,1)}, bf16[2048,384]{1,0:T(8,128)(2,1)}, u32[]{:S(2)}, u32[]{:S(2)}) collective-permute-start(bf16[2048,384]{1,0:T(8,128)(2,1)} %convolution_convert_fusion.7), channel_id=1, source_target_pairs={{0,254},{2,0},{4,2},{6,4},{8,6},{10,8},{12,10},{14,12},{16,14},{18... | collective-permute-start | bytes 4718600 | tf_op jit(solution)/shard_map/ppermute | solution.py:10
  238.0 3.2 copy-start.14
  238.0 38.4 %collective-permute-start.11 = (bf16[384,2048]{1,0:T(8,128)(2,1)S(1)}, bf16[384,2048]{1,0:T(8,128)(2,1)}, u32[]{:S(2)}, u32[]{:S(2)}) collective-permute-start(bf16[384,2048]{1,0:T(8,128)(2,1)S(1)} %convolution_convert_fusion), channel_id=1, source_target_pairs={{0,252},{2,254},{4,0},{6,2},{8,4},{10,6},{12,8},{14,10},{16,12},{1... | collective-permute-start | bytes 4718600 | tf_op jit(solution)/shard_map/ppermute | solution.py:10
  240.1 3.8 copy-start.17
  240.1 68.2 %collective-permute-start.7 = (bf16[2048,384]{1,0:T(8,128)(2,1)}, bf16[2048,384]{1,0:T(8,128)(2,1)}, u32[]{:S(2)}, u32[]{:S(2)}) collective-permute-start(bf16[2048,384]{1,0:T(8,128)(2,1)} %convolution_convert_fusion.6), channel_id=1, source_target_pairs={{0,252},{2,254},{4,0},{6,2},{8,4},{10,6},{12,8},{14,10},{16,12},{1... | collective-permute-start | bytes 4718600 | tf_op jit(solution)/shard_map/ppermute | solution.py:10
  243.0 33.4 %copy-start.11 = (bf16[128,2048]{1,0:T(8,128)(2,1)S(1)}, bf16[128,2048]{1,0:T(8,128)(2,1)}, u32[]{:S(2)}) copy-start(bf16[128,2048]{1,0:T(8,128)(2,1)} %gather_fusion.6) | copy-start | bytes 1572868
  243.0 125.5 %collective-permute-start.8 = (bf16[2048,384]{1,0:T(8,128)(2,1)}, bf16[2048,384]{1,0:T(8,128)(2,1)}, u32[]{:S(2)}, u32[]{:S(2)}) collective-permute-start(bf16[2048,384]{1,0:T(8,128)(2,1)} %convolution_convert_fusion.4), channel_id=1, source_target_pairs={{0,254},{2,0},{4,2},{6,4},{8,6},{10,8},{12,10},{14,12},{16,14},{18... | collective-permute-start | bytes 4718600 | tf_op jit(solution)/shard_map/ppermute | solution.py:10
  260.8 1.1 copy-start.12
  262.0 106.6 %collective-permute-start.9 = (bf16[2048,384]{1,0:T(8,128)(2,1)}, bf16[2048,384]{1,0:T(8,128)(2,1)}, u32[]{:S(2)}, u32[]{:S(2)}) collective-permute-start(bf16[2048,384]{1,0:T(8,128)(2,1)} %convolution_convert_fusion.3), channel_id=1, source_target_pairs={{0,252},{2,254},{4,0},{6,2},{8,4},{10,6},{12,8},{14,10},{16,12},{1... | collective-permute-start | bytes 4718600 | tf_op jit(solution)/shard_map/ppermute | solution.py:10
  276.4 31.9 %copy-start.1 = (bf16[128,2048]{1,0:T(8,128)(2,1)S(1)}, bf16[128,2048]{1,0:T(8,128)(2,1)}, u32[]{:S(2)}) copy-start(bf16[128,2048]{1,0:T(8,128)(2,1)} %gather_fusion.1) | copy-start | bytes 1572868
  276.4 31.9 %copy-start.23 = (bf16[128,384]{1,0:T(8,128)(2,1)S(1)}, bf16[128,384]{1,0:T(8,128)(2,1)}, u32[]{:S(2)}) copy-start(bf16[128,384]{1,0:T(8,128)(2,1)} %copy-done.22) | copy-start | bytes 294916
  280.2 88.3 %copy-start.21 = (bf16[128,384]{1,0:T(8,128)(2,1)S(1)}, bf16[128,384]{1,0:T(8,128)(2,1)}, u32[]{:S(2)}) copy-start(bf16[128,384]{1,0:T(8,128)(2,1)} %copy-done.20) | copy-start | bytes 294916
Sparse Core Ops, SparseCore 0:
  9.8 75.3 all-gather.3
  87.0 33.1 all-gather.5
  203.6 16.1 reduce-scatter.9
  222.1 49.4 reduce-scatter.7
  273.9 200.8 reduce-scatter.5
where the time goes:
time: 492 us; the launch traced here: 484 us
  waiting for transfers between devices  295 us (60%)
  matrix products  64.1 us (13%)
  other arithmetic  49.5 us (10%)
  starting transfers between devices  28.4 us (6%)
  local copies, waits for them, and re-layouts  27.2 us (6%)
  between operations  14.5 us (3%)
  blocking collectives  4.95 us (1%)
    reduce_scatter x1, waiting for transfers between devices, on_device(): lax.psum_scatter(mixed_acc[:group_size], 'dp', scatter_dimension=0, tiled...  100 us
    ppermute x12, waiting for transfers between devices, shifted(): return lax.ppermute(value, axis, pairs)  99.8 us
    all_gather x1, waiting for transfers between devices, on_device(): lax.all_gather(tokens, 'dp', axis=0, tiled=True)  62.3 us
    all_gather x1, waiting for transfers between devices, on_device(): lax.all_gather(cotangent, 'dp', axis=0, tiled=True)  31.7 us
    ppermute x12, starting transfers between devices, shifted(): return lax.ppermute(value, axis, pairs)  28.2 us
    scatter-add x3, other arithmetic, on_device(): gate_acc = gate_acc.at[list_rows, cycle_step].add(results[2])  20.8 us
    scatter-add x3, other arithmetic, on_device(): mixed_acc = mixed_acc.at[list_rows].add(results[0])  12 us
    scatter-add x3, other arithmetic, on_device(): input_acc = input_acc.at[list_rows].add(results[1])  11.8 us
  transfers between devices with their start and end apart: 17, of which 7 were waited for; matrix products, arithmetic and copies ran while one was open for 25% of the time, Pallas kernels for 0%

commit v1 on v0

v1 whole, which is shorter than its diff:
```python
import jax
import jax.numpy as jnp
from jax import lax
from jax.sharding import PartitionSpec as P

BF = jnp.bfloat16
F32 = jnp.float32


def shifted(value, axis, steps):
    count = lax.axis_size(axis)
    pairs = [(source, (source + steps) % count) for source in range(count)]
    return lax.ppermute(value, axis, pairs)


def on_device(tokens, cotangent, gate_probs, slot_rows, w_gate, w_up, w_down):
    half = lax.axis_index("dp")
    own = tokens.shape[0]
    group_x = lax.all_gather(tokens, "dp", axis=0, tiled=True)
    group_dy = lax.all_gather(cotangent, "dp", axis=0, tiled=True)
    group_gate = lax.all_gather(gate_probs, "dp", axis=0, tiled=True)
    cycle, cap = slot_rows.shape
    group = group_x.shape[0]
    names = slot_rows[:, :, None] == lax.broadcasted_iota(jnp.int32, (1, 1, group), 2)
    picks = names.astype(BF)
    rows_x = jnp.einsum("sct,td->scd", picks, group_x, preferred_element_type=F32).astype(BF)
    rows_dy = jnp.einsum("sct,td->scd", picks, group_dy, preferred_element_type=F32).astype(BF)
    rows_gate = jnp.einsum("sct,ts->sc", picks, group_gate, preferred_element_type=F32).astype(BF)
    lists_x, lists_dy, lists_gate = [rows_x[0]], [rows_dy[0]], [rows_gate[0]]
    for step in range(1, cycle):
        lists_x.append(shifted(rows_x[step], "blk", -step))
        lists_dy.append(shifted(rows_dy[step], "blk", -step))
        lists_gate.append(shifted(rows_gate[step], "blk", -step))
    x = jnp.concatenate(lists_x, axis=0)
    dy = jnp.concatenate(lists_dy, axis=0)
    gate = jnp.concatenate(lists_gate, axis=0).astype(F32)[:, None]
    w_g, w_u, w_d = w_gate[0], w_up[0], w_down[0]
    pre_gate = jnp.dot(x, w_g, preferred_element_type=F32)
    pre_up = jnp.dot(x, w_u, preferred_element_type=F32)
    back = jnp.einsum("cd,hd->ch", dy, w_d, preferred_element_type=F32)
    sig = jax.nn.sigmoid(pre_gate)
    active = pre_gate * sig
    hidden = active * pre_up
    gate_part = jnp.sum(hidden * back, axis=1)
    hidden_w = (hidden * gate).astype(BF)
    hidden_grad = back * gate
    pgg = (hidden_grad * pre_up * sig * (1.0 + pre_gate * (1.0 - sig))).astype(BF)
    pug = (hidden_grad * active).astype(BF)
    weighted = jnp.dot(hidden_w, w_d, preferred_element_type=F32).astype(BF)
    in_grad = jnp.einsum("ch,dh->cd", pgg, w_g, preferred_element_type=F32)
    in_grad = in_grad + jnp.einsum("ch,dh->cd", pug, w_u, preferred_element_type=F32)
    in_grad = in_grad.astype(BF)
    out_w, out_i, out_g = [weighted[:cap]], [in_grad[:cap]], [gate_part[:cap]]
    for step in range(1, cycle):
        rows = slice(step * cap, (step + 1) * cap)
        out_w.append(shifted(weighted[rows], "blk", step))
        out_i.append(shifted(in_grad[rows], "blk", step))
        out_g.append(shifted(gate_part[rows], "blk", step))
    d_gate = jnp.einsum("cd,ch->dh", x, pgg, preferred_element_type=F32).astype(BF)
    d_up = jnp.einsum("cd,ch->dh", x, pug, preferred_element_type=F32).astype(BF)
    d_down = jnp.einsum("ch,cd->hd", hidden_w, dy, preferred_element_type=F32).astype(BF)
    back_w = jnp.concatenate(out_w, axis=0)
    back_i = jnp.concatenate(out_i, axis=0)
    flat = picks.reshape(cycle * cap, group)
    mixed = jnp.einsum("ct,cd->td", flat, back_w, preferred_element_type=F32)
    input_grad = jnp.einsum("ct,cd->td", flat, back_i, preferred_element_type=F32)
    gate_grad = jnp.stack(
        [jnp.sum(jnp.where(names[s], out_g[s][:, None], 0.0), axis=0) for s in range(cycle)], axis=1
    )

    def summed(full, kind):
        mine = lax.dynamic_slice_in_dim(full, half * own, own, 0)
        other = lax.dynamic_slice_in_dim(full, (1 - half) * own, own, 0)
        arrived = lax.ppermute(other.astype(kind), "dp", [(0, 1), (1, 0)])
        return mine + arrived.astype(F32)

    return (
        summed(mixed, BF).astype(BF),
        summed(input_grad, BF).astype(BF),
        summed(gate_grad, F32),
        d_gate[None],
        d_up[None],
        d_down[None],
    )


def solution(mesh):
    in_specs = (
        P(("blk", "dp"), None),
        P(("blk", "dp"), None),
        P(("blk", "dp"), None),
        P("blk", None),
        P("blk", None, "dp"),
        P("blk", None, "dp"),
        P("blk", "dp", None),
    )
    out_specs = (
        P(("blk", "dp"), None),
        P(("blk", "dp"), None),
        P(("blk", "dp"), None),
        P("blk", None, "dp"),
        P("blk", None, "dp"),
        P("blk", "dp", None),
    )
    return jax.shard_map(
        on_device, mesh=mesh, in_specs=in_specs, out_specs=out_specs, check_vma=False
    )
```

time: 492 us -> 201 us (0.41); the launches traced: 484 us -> 201 us
  waiting for transfers between devices: 295 us -> 102 us
  other arithmetic: 49.5 us -> 3.09 us
  matrix products: 64.1 us -> 25.4 us
  local copies, waits for them, and re-layouts: 27.2 us -> 1 us
  starting transfers between devices: 28.4 us -> 49.6 us
    reduce_scatter x2 -> x0, waiting for transfers between devices: 100 us -> none  [the longest x1 100 us: on_device(): lax.psum_scatter(mixed_acc[:group_size], 'dp', scatter_dimension=0, tiled...]
    ppermute x12, waiting for transfers between devices: 99.8 us -> 26.9 us  [shifted(): return lax.ppermute(value, axis, pairs)]
    all_gather x2, waiting for transfers between devices: 94 us -> 46.8 us  [the longest x1 26.1 us: on_device(): group_dy = lax.all_gather(cotangent, 'dp', axis=0, tiled=True)]
    scatter-add x9 -> x0, other arithmetic: 44.6 us -> none  [the longest x3 20.8 us: on_device(): gate_acc = gate_acc.at[list_rows, cycle_step].add(results[2])]
    dot_general x27 -> x14, matrix products: 64.1 us -> 25.4 us  [the longest x1 3.54 us: on_device(): jnp.einsum('cd,ch->dh', x, pgg, preferred_element_type=F32).astype(BF)]
    ppermute x0 -> x3, waiting for transfers between devices: none -> 26.9 us  [summed(): arrived = lax.ppermute(other.astype(kind), 'dp', [(0, 1), (1, 0)])]
    gather x9 -> x0, local copies, waits for them, and re-layouts: 15 us -> none  [the longest x3 5.21 us: on_device(): padded_dy[list_rows]]
    ppermute x12, starting transfers between devices: 28.2 us -> 41.3 us  [shifted(): return lax.ppermute(value, axis, pairs)]
  transfers between devices with their start and end apart: 17 -> 17, of which waited for: 7 -> 8; matrix products, arithmetic and copies ran while one was open for 25% -> 13% of each run, Pallas kernels for 0% -> 0%
where the time goes in v1:
time: 201 us
  waiting for transfers between devices  102 us (51%)
  starting transfers between devices  49.6 us (25%)
  matrix products  25.4 us (13%)
  between operations  14.3 us (7%)
  blocking collectives  5.47 us (3%)
  other arithmetic  3.09 us (2%)
    ppermute x12, starting transfers between devices, shifted(): return lax.ppermute(value, axis, pairs)  41.3 us
    ppermute x3, waiting for transfers between devices, summed(): arrived = lax.ppermute(other.astype(kind), 'dp', [(0, 1), (1, 0)])  26.9 us
    ppermute x12, waiting for transfers between devices, shifted(): return lax.ppermute(value, axis, pairs)  26.9 us
    all_gather x1, waiting for transfers between devices, on_device(): group_dy = lax.all_gather(cotangent, 'dp', axis=0, tiled=True)  26.1 us
    all_gather x1, waiting for transfers between devices, on_device(): group_x = lax.all_gather(tokens, 'dp', axis=0, tiled=True)  20.7 us
    ppermute x3, starting transfers between devices, summed(): arrived = lax.ppermute(other.astype(kind), 'dp', [(0, 1), (1, 0)])  8.21 us
    all_gather x1, blocking collectives, on_device(): group_gate = lax.all_gather(gate_probs, 'dp', axis=0, tiled=True)  5.47 us
  transfers between devices with their start and end apart: 17, of which 8 were waited for; matrix products, arithmetic and copies ran while one was open for 13% of the time, Pallas kernels for 0%

profile of v1, /device:TPU:1, one launch (start us, length us, event | category | flops | bytes accessed | tf_op | source)
XLA Modules:
  0.0 200.9 jit_solution(9624781532558431168)
XLA Ops:
  7.2 0.0 copy-start
  7.2 0.0 all-gather.4.cloned.1.call-start
  7.2 0.7 all-gather.4.cloned.1.call-update
  7.9 0.0 all-gather.6.cloned.1.call-start
  8.0 0.7 all-gather.6.cloned.1.call-update
  8.7 5.5 %all-gather = bf16[2,192,3]{1,2,0:T(4,128)(2,1)S(1)} all-gather(bf16[1,192,3]{1,2,0:T(4,128)(2,1)S(1)} %bitcast.76), channel_id=1, replica_groups=mesh['blk'=128,'dp'=2] {'dp'}, dimensions={0}, use_global_device_ids=true | all-gather | bytes 3456 | tf_op jit(solution)/shard_map/all_gather | solution.py:21
  14.2 0.1 reshape.49
  14.3 0.3 fusion.28
  14.6 8.9 %collective-permute-start.3 = (bf16[128]{0:T(256)(128)(2,1)S(1)}, bf16[128]{0:T(256)(128)(2,1)S(1)}, u32[]{:S(2)}, u32[]{:S(2)}) collective-permute-start(bf16[128]{0:T(256)(128)(2,1)S(1)} %get-tuple-element.29), channel_id=1, source_target_pairs={{0,252},{2,254},{4,0},{6,2},{8,4},{10,6},{12,8},{14,10},{16,12},{1... | collective-permute-start | bytes 776 | tf_op jit(solution)/shard_map/ppermute | solution.py:13
  23.5 2.1 %collective-permute-start.2 = (bf16[128]{0:T(256)(128)(2,1)S(1)}, bf16[128]{0:T(256)(128)(2,1)S(1)}, u32[]{:S(2)}, u32[]{:S(2)}) collective-permute-start(bf16[128]{0:T(256)(128)(2,1)S(1)} %get-tuple-element.30), channel_id=1, source_target_pairs={{0,254},{2,0},{4,2},{6,4},{8,6},{10,8},{12,10},{14,12},{16,14},{18... | collective-permute-start | bytes 776 | tf_op jit(solution)/shard_map/ppermute | solution.py:13
  25.6 0.1 iota_compare_fusion
  25.8 0.0 collective-permute-done.3
  25.8 0.7 collective-permute-done.2
  26.5 20.7 %all-gather.4.cloned.1.call-done = bf16[384,2048]{1,0:T(8,128)(2,1)} async-done(((bf16[192,2048]{1,0:T(8,128)(2,1)}), bf16[384,2048]{1,0:T(8,128)(2,1)}) %all-gather.4.cloned.1.call-update) | async-done | bytes 1572880 | tf_op jit(solution)/shard_map/all_gather | solution.py:19
  47.3 2.4 %convolution_convert_fusion.5 = bf16[3,128,2048]{2,1,0:T(8,128)(2,1)S(1)} fusion(bf16[384,2048]{1,0:T(8,128)(2,1)} %all-gather.4.cloned.1.call-done, s32[3,128]{1,0:T(4,128)S(1)} %copy-done.3), kind=kOutput, calls=%fused_computation.6 | convolution fusion | flops 604913664 | bytes 3147264 | tf_op jit(solution)/shard_map/sct,td->scd/dot_general | solution.py:26
  49.7 0.2 slice_bitcast_fusion.5
  49.9 5.3 %collective-permute-start.1 = (bf16[128,2048]{1,0:T(8,128)(2,1)S(1)}, bf16[128,2048]{1,0:T(8,128)(2,1)}, u32[]{:S(2)}, u32[]{:S(2)}) collective-permute-start(bf16[128,2048]{1,0:T(8,128)(2,1)S(1)} %get-tuple-element.21), channel_id=1, source_target_pairs={{0,252},{2,254},{4,0},{6,2},{8,4},{10,6},{12,8},{14,10},{16,12},{1... | collective-permute-start | bytes 1572872 | tf_op jit(solution)/shard_map/ppermute | solution.py:13
  55.1 1.1 collective-permute-start
  56.3 26.1 %all-gather.6.cloned.1.call-done = bf16[384,2048]{1,0:T(8,128)(2,1)} async-done(((bf16[192,2048]{1,0:T(8,128)(2,1)}), bf16[384,2048]{1,0:T(8,128)(2,1)}) %all-gather.6.cloned.1.call-update) | async-done | bytes 1572880 | tf_op jit(solution)/shard_map/all_gather | solution.py:20
  82.3 2.4 %convolution_convert_fusion.3 = bf16[3,128,2048]{2,1,0:T(8,128)(2,1)S(1)} fusion(bf16[384,2048]{1,0:T(8,128)(2,1)} %all-gather.6.cloned.1.call-done, s32[3,128]{1,0:T(4,128)S(1)} %copy-done.3), kind=kOutput, calls=%fused_computation.4 | convolution fusion | flops 604913664 | bytes 3147264 | tf_op jit(solution)/shard_map/sct,td->scd/dot_general | solution.py:27
  84.8 0.0 copy-start.2
  84.8 0.1 slice_bitcast_fusion.2
  84.9 10.9 %collective-permute-start.8 = (bf16[128,2048]{1,0:T(8,128)(2,1)S(1)}, bf16[128,2048]{1,0:T(8,128)(2,1)S(1)}, u32[]{:S(2)}, u32[]{:S(2)}) collective-permute-start(bf16[128,2048]{1,0:T(8,128)(2,1)S(1)} %get-tuple-element.15), channel_id=1, source_target_pairs={{0,252},{2,254},{4,0},{6,2},{8,4},{10,6},{12,8},{14,10},{16,12},{1... | collective-permute-start | bytes 1572872 | tf_op jit(solution)/shard_map/ppermute | solution.py:13
  95.8 0.8 collective-permute-start.7
  96.5 0.0 collective-permute-done.1
  96.5 0.0 collective-permute-done
  96.6 0.0 copy-start.1
  96.6 2.4 %fusion.20 = f32[384,384]{0,1:T(8,128)S(1)} fusion(bf16[1,2048,384]{2,1,0:T(8,128)(2,1)S(1)} %copy-done.2, bf16[128,2048]{1,0:T(8,128)(2,1)} %collective-permute-done.1, bf16[128,2048]{1,0:T(8,128)(2,1)} %collective-permute-done, bf16[128,2048]{1,0:T(8,128)(2,1)S(1)} %get-tuple-element.20), kind=kOutput, calls=%fused_computation.29 | convolution fusion | flops 608698368 | bytes 3735552 | tf_op jit(solution)/shard_map/dot_general | solution.py:39
  98.9 2.2 %fusion.24 = f32[384,384]{0,1:T(8,128)S(1)} fusion(bf16[1,2048,384]{2,1,0:T(8,128)(2,1)S(1)} %copy-done.1, bf16[128,2048]{1,0:T(8,128)(2,1)} %collective-permute-done.1, bf16[128,2048]{1,0:T(8,128)(2,1)} %collective-permute-done, bf16[128,2048]{1,0:T(8,128)(2,1)S(1)} %get-tuple-element.20), kind=kOutput, calls=%fused_computation.33 | convolution fusion | flops 608698368 | bytes 3735552 | tf_op jit(solution)/shard_map/dot_general | solution.py:38
  101.2 5.3 %collective-permute-done.8 = bf16[128,2048]{1,0:T(8,128)(2,1)S(1)} collective-permute-done((bf16[128,2048]{1,0:T(8,128)(2,1)S(1)}, bf16[128,2048]{1,0:T(8,128)(2,1)S(1)}, u32[]{:S(2)}, u32[]{:S(2)}) %collective-permute-start.8) | collective-permute-done | bytes 524320 | tf_op jit(solution)/shard_map/ppermute | solution.py:13
  106.5 1.2 multiply_reduce_fusion
  107.8 1.0 convolution_convert_fusion.4
  108.8 0.1 fusion.39
  108.9 0.1 collective-permute-start.5
  109.0 2.5 %collective-permute-start.4 = (bf16[128,2048]{1,0:T(8,128)(2,1)S(1)}, bf16[128,2048]{1,0:T(8,128)(2,1)S(1)}, u32[]{:S(2)}, u32[]{:S(2)}) collective-permute-start(bf16[128,2048]{1,0:T(8,128)(2,1)S(1)} %get-tuple-element.19), channel_id=1, source_target_pairs={{0,2},{2,4},{4,6},{6,8},{8,10},{10,12},{12,14},{14,16},{16,18},{18... | collective-permute-start | bytes 1572872 | tf_op jit(solution)/shard_map/ppermute | solution.py:13
  111.5 1.0 fusion.22
  112.5 1.0 add_convert_fusion
  113.6 0.2 fusion.38
  113.7 5.0 %collective-permute-start.10 = (bf16[128,2048]{1,0:T(8,128)(2,1)S(1)}, bf16[128,2048]{1,0:T(8,128)(2,1)S(1)}, u32[]{:S(2)}, u32[]{:S(2)}) collective-permute-start(bf16[128,2048]{1,0:T(8,128)(2,1)S(1)} %get-tuple-element.12), channel_id=1, source_target_pairs={{0,4},{2,6},{4,8},{6,10},{8,12},{10,14},{12,16},{14,18},{16,20},{1... | collective-permute-start | bytes 1572872 | tf_op jit(solution)/shard_map/ppermute | solution.py:13
  118.7 3.6 %collective-permute-start.13 = (f32[128]{0:T(128)S(1)}, f32[128]{0:T(128)S(1)}, u32[]{:S(2)}, u32[]{:S(2)}) collective-permute-start(f32[128]{0:T(128)S(1)} %get-tuple-element.26), channel_id=1, source_target_pairs={{0,4},{2,6},{4,8},{6,10},{8,12},{10,14},{12,16},{14,18},{16,20},{1... | collective-permute-start | bytes 1544 | tf_op jit(solution)/shard_map/ppermute | solution.py:13
  122.3 1.1 collective-permute-start.12
  123.4 3.5 %fusion = bf16[1,2048,384]{2,1,0:T(8,128)(2,1)} fusion(bf16[384,384]{0,1:T(8,128)(2,1)S(1)} %get-tuple-element.10, bf16[128,2048]{1,0:T(8,128)(2,1)} %collective-permute-done.1, bf16[128,2048]{1,0:T(8,128)(2,1)} %collective-permute-done, bf16[128,2048]{1,0:T(8,128)(2,1)S(1)} %get-tuple-element.20), kind=kOutput, calls=%fused_computation.7 | convolution fusion | flops 609484800 | bytes 3440640 | tf_op jit(solution)/shard_map/cd,ch->dh/dot_general | solution.py:59
  126.9 3.5 %fusion.1 = bf16[1,2048,384]{2,1,0:T(8,128)(2,1)} fusion(bf16[384,384]{0,1:T(8,128)(2,1)S(1)} %get-tuple-element.24, bf16[128,2048]{1,0:T(8,128)(2,1)} %collective-permute-done.1, bf16[128,2048]{1,0:T(8,128)(2,1)} %collective-permute-done, bf16[128,2048]{1,0:T(8,128)(2,1)S(1)} %get-tuple-element.20), kind=kOutput, calls=%fused_computation.8 | convolution fusion | flops 609484800 | bytes 3440640 | tf_op jit(solution)/shard_map/cd,ch->dh/dot_general | solution.py:60
  130.5 20.4 %collective-permute-done.13 = f32[128]{0:T(128)S(1)} collective-permute-done((f32[128]{0:T(128)S(1)}, f32[128]{0:T(128)S(1)}, u32[]{:S(2)}, u32[]{:S(2)}) %collective-permute-start.13) | collective-permute-done | bytes 544 | tf_op jit(solution)/shard_map/ppermute | solution.py:13
  150.8 0.0 collective-permute-start.9
  150.8 0.0 collective-permute-done.12
  150.8 0.2 select_reduce_fusion.2
  151.0 0.1 constant_dynamic-slice_fusion
  151.1 4.0 %collective-permute-start.14 = (f32[192,3]{0,1:T(4,128)S(1)}, f32[192,3]{0,1:T(4,128)S(1)}, u32[]{:S(2)}, u32[]{:S(2)}) collective-permute-start(f32[192,3]{0,1:T(4,128)S(1)} %constant_dynamic-slice_fusion), channel_id=1, source_target_pairs={{0,1},{1,0},{2,3},{3,2},{4,5},{5,4},{6,7},{7,6},{8,9},{9,8},{10,11... | collective-permute-start | bytes 6920 | tf_op jit(solution)/shard_map/ppermute | solution.py:74
  155.1 0.0 collective-permute-done.5
  155.1 0.0 collective-permute-done.4
  155.1 1.1 fusion.3
  156.2 0.1 dynamic-slice_convert_fusion.1
  156.4 0.1 collective-permute-start.6
  156.5 0.5 collective-permute-done.9
  156.9 1.1 fusion.9
  158.0 0.1 dynamic-slice_convert_fusion
  158.2 4.1 %collective-permute-start.11 = (bf16[192,2048]{1,0:T(8,128)(2,1)S(1)}, bf16[192,2048]{1,0:T(8,128)(2,1)S(1)}, u32[]{:S(2)}, u32[]{:S(2)}) collective-permute-start(bf16[192,2048]{1,0:T(8,128)(2,1)S(1)} %dynamic-slice_convert_fusion), channel_id=1, source_target_pairs={{0,1},{1,0},{2,3},{3,2},{4,5},{5,4},{6,7},{7,6},{8,9},{9,8},{10,11... | collective-permute-start | bytes 2359304 | tf_op jit(solution)/shard_map/ppermute | solution.py:74
  162.2 2.1 %fusion.2 = bf16[1,384,2048]{2,1,0:T(8,128)(2,1)} fusion(bf16[384,384]{0,1:T(8,128)(2,1)S(1)} %get-tuple-element.23, bf16[128,2048]{1,0:T(8,128)(2,1)S(1)} %collective-permute-done.8, bf16[128,2048]{1,0:T(8,128)(2,1)S(1)} %collective-permute-done.7, bf16[128,2048]{1,0:T(8,128)(2,1)S(1)} %get-tuple-element.14), kind=kOutput, calls=%fused_computation.9 | convolution fusion | flops 609484800 | bytes 3440640 | tf_op jit(solution)/shard_map/ch,cd->hd/dot_general | solution.py:61
  164.4 0.7 dynamic-slice_add_fusion
  165.0 11.1 %collective-permute-done.6 = bf16[192,2048]{1,0:T(8,128)(2,1)S(1)} collective-permute-done((bf16[192,2048]{1,0:T(8,128)(2,1)S(1)}, bf16[192,2048]{1,0:T(8,128)(2,1)S(1)}, u32[]{:S(2)}, u32[]{:S(2)}) %collective-permute-start.6) | collective-permute-done | bytes 786464 | tf_op jit(solution)/shard_map/ppermute | solution.py:74
  176.2 1.1 add_convert_fusion.2
  177.2 15.8 %collective-permute-done.11 = bf16[192,2048]{1,0:T(8,128)(2,1)S(1)} collective-permute-done((bf16[192,2048]{1,0:T(8,128)(2,1)S(1)}, bf16[192,2048]{1,0:T(8,128)(2,1)S(1)}, u32[]{:S(2)}, u32[]{:S(2)}) %collective-permute-start.11) | collective-permute-done | bytes 786464 | tf_op jit(solution)/shard_map/ppermute | solution.py:74
  193.0 1.1 add_convert_fusion.1
  (19 shorter events, 0.1 us)
Async XLA Ops:
  7.2 99.4 %copy-start = (bf16[1,384,2048]{2,1,0:T(8,128)(2,1)S(1)}, bf16[1,384,2048]{2,1,0:T(8,128)(2,1)}, u32[]{:S(2)}) copy-start(bf16[1,384,2048]{2,1,0:T(8,128)(2,1)} %param.13) | copy-start | bytes 4718596
  7.2 1.5 copy-start.4
  7.2 7.1 %copy-start.3 = (s32[3,128]{1,0:T(4,128)S(1)}, s32[3,128]{1,0:T(4,128)}, u32[]{:S(2)}) copy-start(s32[3,128]{1,0:T(4,128)} %param.10) | copy-start | bytes 4612
  7.2 40.1 %all-gather.4.cloned.1.call-start = ((), (), s32[]{:S(2)}) async-start(), calls=%async_computation | async-start | bytes 2359296 | tf_op jit(solution)/shard_map/all_gather | solution.py:19
  7.9 74.4 %all-gather.6.cloned.1.call-start = ((), (), s32[]{:S(2)}) async-start(), calls=%async_computation.1 | async-start | bytes 2359296 | tf_op jit(solution)/shard_map/all_gather | solution.py:20
  14.6 11.2 %collective-permute-start.3 = (bf16[128]{0:T(256)(128)(2,1)S(1)}, bf16[128]{0:T(256)(128)(2,1)S(1)}, u32[]{:S(2)}, u32[]{:S(2)}) collective-permute-start(bf16[128]{0:T(256)(128)(2,1)S(1)} %get-tuple-element.29), channel_id=1, source_target_pairs={{0,252},{2,254},{4,0},{6,2},{8,4},{10,6},{12,8},{14,10},{16,12},{1... | collective-permute-start | bytes 776 | tf_op jit(solution)/shard_map/ppermute | solution.py:13
  23.5 3.0 %collective-permute-start.2 = (bf16[128]{0:T(256)(128)(2,1)S(1)}, bf16[128]{0:T(256)(128)(2,1)S(1)}, u32[]{:S(2)}, u32[]{:S(2)}) collective-permute-start(bf16[128]{0:T(256)(128)(2,1)S(1)} %get-tuple-element.30), channel_id=1, source_target_pairs={{0,254},{2,0},{4,2},{6,4},{8,6},{10,8},{12,10},{14,12},{16,14},{18... | collective-permute-start | bytes 776 | tf_op jit(solution)/shard_map/ppermute | solution.py:13
  49.9 46.7 %collective-permute-start.1 = (bf16[128,2048]{1,0:T(8,128)(2,1)S(1)}, bf16[128,2048]{1,0:T(8,128)(2,1)}, u32[]{:S(2)}, u32[]{:S(2)}) collective-permute-start(bf16[128,2048]{1,0:T(8,128)(2,1)S(1)} %get-tuple-element.21), channel_id=1, source_target_pairs={{0,252},{2,254},{4,0},{6,2},{8,4},{10,6},{12,8},{14,10},{16,12},{1... | collective-permute-start | bytes 1572872 | tf_op jit(solution)/shard_map/ppermute | solution.py:13
  55.1 41.4 %collective-permute-start = (bf16[128,2048]{1,0:T(8,128)(2,1)S(1)}, bf16[128,2048]{1,0:T(8,128)(2,1)}, u32[]{:S(2)}, u32[]{:S(2)}) collective-permute-start(bf16[128,2048]{1,0:T(8,128)(2,1)S(1)} %get-tuple-element.22), channel_id=1, source_target_pairs={{0,254},{2,0},{4,2},{6,4},{8,6},{10,8},{12,10},{14,12},{16,14},{18... | collective-permute-start | bytes 1572872 | tf_op jit(solution)/shard_map/ppermute | solution.py:13
  84.8 11.8 %copy-start.2 = (bf16[1,2048,384]{2,1,0:T(8,128)(2,1)S(1)}, bf16[1,2048,384]{2,1,0:T(8,128)(2,1)}, u32[]{:S(2)}) copy-start(bf16[1,2048,384]{2,1,0:T(8,128)(2,1)} %param.12) | copy-start | bytes 4718596
  84.9 21.7 %collective-permute-start.8 = (bf16[128,2048]{1,0:T(8,128)(2,1)S(1)}, bf16[128,2048]{1,0:T(8,128)(2,1)S(1)}, u32[]{:S(2)}, u32[]{:S(2)}) collective-permute-start(bf16[128,2048]{1,0:T(8,128)(2,1)S(1)} %get-tuple-element.15), channel_id=1, source_target_pairs={{0,252},{2,254},{4,0},{6,2},{8,4},{10,6},{12,8},{14,10},{16,12},{1... | collective-permute-start | bytes 1572872 | tf_op jit(solution)/shard_map/ppermute | solution.py:13
  95.8 10.8 %collective-permute-start.7 = (bf16[128,2048]{1,0:T(8,128)(2,1)S(1)}, bf16[128,2048]{1,0:T(8,128)(2,1)S(1)}, u32[]{:S(2)}, u32[]{:S(2)}) collective-permute-start(bf16[128,2048]{1,0:T(8,128)(2,1)S(1)} %get-tuple-element.16), channel_id=1, source_target_pairs={{0,254},{2,0},{4,2},{6,4},{8,6},{10,8},{12,10},{14,12},{16,14},{18... | collective-permute-start | bytes 1572872 | tf_op jit(solution)/shard_map/ppermute | solution.py:13
  96.6 2.4 %copy-start.1 = (bf16[1,2048,384]{2,1,0:T(8,128)(2,1)S(1)}, bf16[1,2048,384]{2,1,0:T(8,128)(2,1)}, u32[]{:S(2)}) copy-start(bf16[1,2048,384]{2,1,0:T(8,128)(2,1)} %param.11) | copy-start | bytes 4718596
  108.9 46.2 %collective-permute-start.5 = (bf16[128,2048]{1,0:T(8,128)(2,1)S(1)}, bf16[128,2048]{1,0:T(8,128)(2,1)S(1)}, u32[]{:S(2)}, u32[]{:S(2)}) collective-permute-start(bf16[128,2048]{1,0:T(8,128)(2,1)S(1)} %get-tuple-element.18), channel_id=1, source_target_pairs={{0,4},{2,6},{4,8},{6,10},{8,12},{10,14},{12,16},{14,18},{16,20},{1... | collective-permute-start | bytes 1572872 | tf_op jit(solution)/shard_map/ppermute | solution.py:13
  109.0 46.1 %collective-permute-start.4 = (bf16[128,2048]{1,0:T(8,128)(2,1)S(1)}, bf16[128,2048]{1,0:T(8,128)(2,1)S(1)}, u32[]{:S(2)}, u32[]{:S(2)}) collective-permute-start(bf16[128,2048]{1,0:T(8,128)(2,1)S(1)} %get-tuple-element.19), channel_id=1, source_target_pairs={{0,2},{2,4},{4,6},{6,8},{8,10},{10,12},{12,14},{14,16},{16,18},{18... | collective-permute-start | bytes 1572872 | tf_op jit(solution)/shard_map/ppermute | solution.py:13
  113.7 42.7 %collective-permute-start.10 = (bf16[128,2048]{1,0:T(8,128)(2,1)S(1)}, bf16[128,2048]{1,0:T(8,128)(2,1)S(1)}, u32[]{:S(2)}, u32[]{:S(2)}) collective-permute-start(bf16[128,2048]{1,0:T(8,128)(2,1)S(1)} %get-tuple-element.12), channel_id=1, source_target_pairs={{0,4},{2,6},{4,8},{6,10},{8,12},{10,14},{12,16},{14,18},{16,20},{1... | collective-permute-start | bytes 1572872 | tf_op jit(solution)/shard_map/ppermute | solution.py:13
  118.7 32.1 %collective-permute-start.13 = (f32[128]{0:T(128)S(1)}, f32[128]{0:T(128)S(1)}, u32[]{:S(2)}, u32[]{:S(2)}) collective-permute-start(f32[128]{0:T(128)S(1)} %get-tuple-element.26), channel_id=1, source_target_pairs={{0,4},{2,6},{4,8},{6,10},{8,12},{10,14},{12,16},{14,18},{16,20},{1... | collective-permute-start | bytes 1544 | tf_op jit(solution)/shard_map/ppermute | solution.py:13
  122.3 28.5 %collective-permute-start.12 = (f32[128]{0:T(128)S(1)}, f32[128]{0:T(128)S(1)}, u32[]{:S(2)}, u32[]{:S(2)}) collective-permute-start(f32[128]{0:T(128)S(1)} %get-tuple-element.25), channel_id=1, source_target_pairs={{0,2},{2,4},{4,6},{6,8},{8,10},{10,12},{12,14},{14,16},{16,18},{18... | collective-permute-start | bytes 1544 | tf_op jit(solution)/shard_map/ppermute | solution.py:13
  150.8 6.1 %collective-permute-start.9 = (bf16[128,2048]{1,0:T(8,128)(2,1)S(1)}, bf16[128,2048]{1,0:T(8,128)(2,1)S(1)}, u32[]{:S(2)}, u32[]{:S(2)}) collective-permute-start(bf16[128,2048]{1,0:T(8,128)(2,1)S(1)} %get-tuple-element.13), channel_id=1, source_target_pairs={{0,2},{2,4},{4,6},{6,8},{8,10},{10,12},{12,14},{14,16},{16,18},{18... | collective-permute-start | bytes 1572872 | tf_op jit(solution)/shard_map/ppermute | solution.py:13
  151.1 13.3 %collective-permute-start.14 = (f32[192,3]{0,1:T(4,128)S(1)}, f32[192,3]{0,1:T(4,128)S(1)}, u32[]{:S(2)}, u32[]{:S(2)}) collective-permute-start(f32[192,3]{0,1:T(4,128)S(1)} %constant_dynamic-slice_fusion), channel_id=1, source_target_pairs={{0,1},{1,0},{2,3},{3,2},{4,5},{5,4},{6,7},{7,6},{8,9},{9,8},{10,11... | collective-permute-start | bytes 6920 | tf_op jit(solution)/shard_map/ppermute | solution.py:74
  156.4 19.8 %collective-permute-start.6 = (bf16[192,2048]{1,0:T(8,128)(2,1)S(1)}, bf16[192,2048]{1,0:T(8,128)(2,1)S(1)}, u32[]{:S(2)}, u32[]{:S(2)}) collective-permute-start(bf16[192,2048]{1,0:T(8,128)(2,1)S(1)} %dynamic-slice_convert_fusion.1), channel_id=1, source_target_pairs={{0,1},{1,0},{2,3},{3,2},{4,5},{5,4},{6,7},{7,6},{8,9},{9,8},{10,11... | collective-permute-start | bytes 2359304 | tf_op jit(solution)/shard_map/ppermute | solution.py:74
  158.2 34.9 %collective-permute-start.11 = (bf16[192,2048]{1,0:T(8,128)(2,1)S(1)}, bf16[192,2048]{1,0:T(8,128)(2,1)S(1)}, u32[]{:S(2)}, u32[]{:S(2)}) collective-permute-start(bf16[192,2048]{1,0:T(8,128)(2,1)S(1)} %dynamic-slice_convert_fusion), channel_id=1, source_target_pairs={{0,1},{1,0},{2,3},{3,2},{4,5},{5,4},{6,7},{7,6},{8,9},{9,8},{10,11... | collective-permute-start | bytes 2359304 | tf_op jit(solution)/shard_map/ppermute | solution.py:74
Sparse Core Ops, SparseCore 0:
  9.8 37.4 all-gather.3
  49.1 33.2 all-gather.5

commit v2 on v1

v2 whole, which is shorter than its diff:
```python
import jax
import jax.numpy as jnp
from jax import lax
from jax.experimental import pallas as pl
from jax.experimental.pallas import tpu as pltpu
from jax.sharding import PartitionSpec as P

BF = jnp.bfloat16
F32 = jnp.float32
MESH = pl.DeviceIdType.MESH
CHUNKS = 8


def dot(a, b, ca=1, cb=0):
    return lax.dot_general(a, b, (((ca,), (cb,)), ((), ())), preferred_element_type=F32)


def kernel(
    blocks, tok, cot, gate, slots, w_g, w_u, w_d,
    o_mix, o_in, o_gate, o_dg, o_du, o_dd,
    X, E, S, G, EG, GS, WGU, WD, PICK, PUT, PRE, BACK, PGU, HW, R, RR, GG, GGS, OWN, YS, YR, OUT, DGU, DD,
    ld_x, ld_w, ld_d, ld_g, yf_s, yf_r, yg_s, yg_r, xf_s, xf_r, xg_s, xg_r, xr_s, xr_r, gg_s, gg_r, yr_s, yr_r,
    st_o, st_w, st_d,
):
    nc, _, _, cw = X.shape
    own, cap = tok.shape[0], slots.shape[1]
    hid = WD.shape[1]
    b, h = lax.axis_index("blk"), lax.axis_index("dp")
    peer = (b, 1 - h)
    x8 = lax.rem(b, 8)

    def down(s):
        return lax.rem(b + blocks - s, blocks)

    def up(s):
        return lax.rem(b + s, blocks)

    def down_dev(s, c):
        cross = 1 - lax.div(x8 + 8 - s, 8)
        return (down(s), lax.rem(h + cross * lax.rem(c, 2), 2))

    def up_dev(s, c):
        cross = lax.div(x8 + s, 8)
        return (up(s), lax.rem(h + cross * lax.rem(c, 2), 2))

    def cols(c):
        return pl.ds(pl.multiple_of(c * cw, cw), cw)

    def load_x(k, c):
        return pltpu.make_async_copy((tok, cot)[k].at[:, cols(c)], X.at[c, k, pl.ds(0, own)], ld_x.at[k, c])

    def send_y(k, c):
        return pltpu.make_async_remote_copy(
            (tok, cot)[k].at[:, cols(c)], X.at[c, k, pl.ds(own, own)], yf_s.at[k, c], yf_r.at[k, c],
            device_id=peer, device_id_type=MESH)

    def send_x(s, c):
        return pltpu.make_async_remote_copy(
            S.at[c, s - 1], E.at[c, s], xf_s.at[s - 1, c], xf_r.at[s - 1, c],
            device_id=down_dev(s, c), device_id_type=MESH)

    def send_back(s, c):
        return pltpu.make_async_remote_copy(
            R.at[c, s - 1], RR.at[c, s], xr_s.at[s - 1, c], xr_r.at[s - 1, c],
            device_id=up_dev(s, c), device_id_type=MESH)

    def send_sum(c):
        return pltpu.make_async_remote_copy(
            YS.at[c], YR.at[c], yr_s.at[c], yr_r.at[c], device_id=peer, device_id_type=MESH)

    def send_gate():
        return pltpu.make_async_remote_copy(
            gate, G.at[pl.ds(own, own)], yg_s, yg_r, device_id=peer, device_id_type=MESH)

    def send_list_gate(s):
        return pltpu.make_async_remote_copy(
            GS.at[s - 1], EG.at[s], xg_s.at[s - 1], xg_r.at[s - 1],
            device_id=(down(s), h), device_id_type=MESH)

    def send_gate_grad(s, rel):
        source = GG.at[0, 0] if s == 0 else GGS.at[s - 1]
        target = (up(s), h if rel == 0 else 1 - h)
        return pltpu.make_async_remote_copy(
            source, GG.at[s, rel], gg_s.at[s, rel], gg_r.at[s, rel], device_id=target, device_id_type=MESH)

    routes = [(0, 1), (1, 0), (1, 1), (2, 0), (2, 1)]

    bar = pltpu.get_barrier_semaphore()
    near = [peer] + [(f(s), d) for f in (down, up) for s in (1, 2) for d in (h, 1 - h)]
    for device in near:
        pl.semaphore_signal(bar, inc=1, device_id=device, device_id_type=MESH)
    load_gate = pltpu.make_async_copy(gate, G.at[pl.ds(0, own)], ld_g)
    load_gate.start()

    def begin(c, _):
        load_x(0, c).start()
        load_x(1, c).start()
        return 0

    lax.fori_loop(0, nc, begin, 0)
    pl.semaphore_wait(bar, len(near))
    send_gate().start()

    def cross(c, _):
        send_y(0, c).start()
        send_y(1, c).start()
        return 0

    lax.fori_loop(0, nc, cross, 0)
    load_wg = pltpu.make_async_copy(w_g.at[0], WGU.at[:, pl.ds(0, hid)], ld_w.at[0])
    load_wu = pltpu.make_async_copy(w_u.at[0], WGU.at[:, pl.ds(hid, hid)], ld_w.at[1])
    load_wg.start()
    load_wu.start()

    def load_wd(c):
        return pltpu.make_async_copy(w_d.at[0, :, cols(c)], WD.at[c], ld_d.at[c])

    def begin_d(c, _):
        load_wd(c).start()
        return 0

    lax.fori_loop(0, nc, begin_d, 0)

    for s in range(3):
        row = slots[s : s + 1, :]
        at = lax.broadcasted_iota(jnp.int32, (own, cap), 0)
        mine = jnp.where(row == at + h * own, 1.0, 0.0).astype(F32)
        other = jnp.where(row == at + (1 - h) * own, 1.0, 0.0).astype(F32)
        PUT[0:own, s * cap : (s + 1) * cap] = mine.astype(BF)
        PUT[own : 2 * own, s * cap : (s + 1) * cap] = other.astype(BF)
        both = jnp.concatenate([mine, other], axis=0)
        PICK[s * cap : (s + 1) * cap, :] = both.T.astype(BF)
    PRE[...] = jnp.zeros_like(PRE)
    BACK[...] = jnp.zeros_like(BACK)

    load_gate.wait()
    send_gate().wait_recv()
    for s in (2, 1, 0):
        picked = dot(PICK[s * cap : (s + 1) * cap, :], G[...]).astype(BF)
        if s:
            GS[s - 1] = picked
            send_list_gate(s).start()
        else:
            EG[0] = picked
    load_wg.wait()
    load_wu.wait()

    def project(c):
        send_x(1, c).wait_recv()
        send_x(2, c).wait_recv()
        load_wd(c).wait()
        x = E[c, :, 0].reshape(3 * cap, cw)
        dy = E[c, :, 1].reshape(3 * cap, cw)
        PRE[...] += dot(x, WGU[pl.ds(pl.multiple_of(c * cw, cw), cw), :])
        BACK[...] += dot(dy, WD[c], 1, 1)

    def forward(c, _):
        for k in range(2):
            load_x(k, c).wait()
            send_y(k, c).wait_recv()
        for k in range(2):
            rows = dot(PICK[...], X[c, k]).astype(BF)
            E[c, 0, k] = rows[0:cap]
            S[c, 0, k] = rows[cap : 2 * cap]
            S[c, 1, k] = rows[2 * cap : 3 * cap]
        send_x(2, c).start()
        send_x(1, c).start()

        @pl.when(c > 0)
        def _():
            project(c - 1)

        return 0

    lax.fori_loop(0, nc, forward, 0)
    project(nc - 1)
    send_list_gate(1).wait_recv()
    send_list_gate(2).wait_recv()

    for s in range(3):
        rows = slice(s * cap, (s + 1) * cap)
        gate_col = EG[s].astype(F32)[:, s : s + 1]
        pre_gate = PRE[rows, 0:hid]
        pre_up = PRE[rows, hid : 2 * hid]
        back = BACK[rows, :]
        sig = jax.nn.sigmoid(pre_gate)
        active = pre_gate * sig
        hidden = active * pre_up
        part = jnp.sum(hidden * back, axis=1, keepdims=True)
        part = jnp.broadcast_to(part, (cap, cap)).T[0:8, :]
        if s == 0:
            GG[0, 0] = part
        else:
            GGS[s - 1] = part
        grad = back * gate_col
        HW[rows, :] = (hidden * gate_col).astype(BF)
        PGU[rows, 0:hid] = (grad * pre_up * sig * (1.0 + pre_gate * (1.0 - sig))).astype(BF)
        PGU[rows, hid : 2 * hid] = (grad * active).astype(BF)

    def results(c, _):
        weighted = dot(HW[...], WD[c]).astype(BF)
        in_grad = dot(PGU[...], WGU[pl.ds(pl.multiple_of(c * cw, cw), cw), :], 1, 1).astype(BF)
        for k, value in enumerate((weighted, in_grad)):
            RR[c, 0, k] = value[0:cap]
            R[c, 0, k] = value[cap : 2 * cap]
            R[c, 1, k] = value[2 * cap : 3 * cap]
        send_back(2, c).start()
        send_back(1, c).start()
        return 0

    lax.fori_loop(0, nc, results, 0)
    for s, rel in routes:
        send_gate_grad(s, rel).start()

    def store_w(k, c):
        target = (o_dg, o_du)[k].at[0, pl.ds(pl.multiple_of(c * cw, cw), cw), :]
        return pltpu.make_async_copy(DGU.at[c, :, pl.ds(k * hid, hid)], target, st_w.at[k, c])

    def store_d(c):
        return pltpu.make_async_copy(DD.at[c], o_dd.at[0, :, cols(c)], st_d.at[c])

    def weight_grads(c, _):
        x = E[c, :, 0].reshape(3 * cap, cw)
        dy = E[c, :, 1].reshape(3 * cap, cw)
        DGU[c] = dot(x, PGU[...], 0, 0).astype(BF)
        DD[c] = dot(HW[...], dy, 0, 0).astype(BF)
        store_w(0, c).start()
        store_w(1, c).start()
        store_d(c).start()
        return 0

    lax.fori_loop(0, nc, weight_grads, 0)

    def store_out(k, c):
        return pltpu.make_async_copy(OUT.at[c, k], (o_mix, o_in)[k].at[:, cols(c)], st_o.at[k, c])

    def finish(c):
        send_sum(c).wait_recv()
        for k in range(2):
            OUT[c, k] = (OWN[c, k] + YR[c, k].astype(F32)).astype(BF)
            store_out(k, c).start()

    def collect(c, _):
        send_back(1, c).wait_recv()
        send_back(2, c).wait_recv()
        for k in range(2):
            rows = RR[c, :, k].reshape(3 * cap, cw)
            total = dot(PUT[...], rows)
            YS[c, k] = total[own : 2 * own].astype(BF)
            OWN[c, k] = total[0:own]
        send_sum(c).start()

        @pl.when(c > 1)
        def _():
            finish(c - 2)

        return 0

    lax.fori_loop(0, nc, collect, 0)

    for s, rel in routes:
        send_gate_grad(s, rel).wait_recv()
    lane = lax.broadcasted_iota(jnp.int32, (own, cap), 1)
    grads = jnp.zeros((own, cap), F32)
    for s in range(3):
        row = GG[s, 0][0:1, :] + GG[s, 1][0:1, :]
        named = PUT[0:own, s * cap : (s + 1) * cap].astype(F32)
        column = jnp.sum(jnp.where(named > 0.5, jnp.broadcast_to(row, (own, cap)), 0.0), axis=1, keepdims=True)
        grads = jnp.where(lane == s, column, grads)
    o_gate[...] = grads

    finish(nc - 2)
    finish(nc - 1)

    send_gate().wait_send()
    for s in (1, 2):
        send_list_gate(s).wait_send()
    for s, rel in routes:
        send_gate_grad(s, rel).wait_send()

    def drain(c, _):
        for k in range(2):
            send_y(k, c).wait_send()
            store_w(k, c).wait()
            store_out(k, c).wait()
        for s in (1, 2):
            send_x(s, c).wait_send()
            send_back(s, c).wait_send()
        send_sum(c).wait_send()
        store_d(c).wait()
        return 0

    lax.fori_loop(0, nc, drain, 0)


def on_device(tokens, cotangent, gate_probs, slot_rows, w_gate, w_up, w_down):
    own, width = tokens.shape
    cycle, cap = slot_rows.shape
    hid = w_gate.shape[2]
    nc, cw = CHUNKS, width // CHUNKS
    group, lists = 2 * own, cycle * cap
    blocks = lax.axis_size("blk")
    padded = jnp.pad(gate_probs, ((0, 0), (0, cap - cycle)))
    dma = pltpu.SemaphoreType.DMA
    vmem = pltpu.VMEM
    any_space = pl.BlockSpec(memory_space=pl.ANY)
    in_vmem = pl.BlockSpec(memory_space=pltpu.VMEM)

    def body(*refs):
        kernel(blocks, *refs)

    outs = pl.pallas_call(
        body,
        out_shape=(
            jax.ShapeDtypeStruct((own, width), BF),
            jax.ShapeDtypeStruct((own, width), BF),
            jax.ShapeDtypeStruct((own, cap), F32),
            jax.ShapeDtypeStruct(w_gate.shape, BF),
            jax.ShapeDtypeStruct(w_up.shape, BF),
            jax.ShapeDtypeStruct(w_down.shape, BF),
        ),
        in_specs=[any_space, any_space, any_space, in_vmem, any_space, any_space, any_space],
        out_specs=(any_space, any_space, in_vmem, any_space, any_space, any_space),
        scratch_shapes=[
            vmem((nc, 2, group, cw), BF),
            vmem((nc, cycle, 2, cap, cw), BF),
            vmem((nc, cycle - 1, 2, cap, cw), BF),
            vmem((group, cap), BF),
            vmem((cycle, cap, cap), BF),
            vmem((cycle - 1, cap, cap), BF),
            vmem((width, 2 * hid), BF),
            vmem((nc, hid, cw), BF),
            vmem((lists, group), BF),
            vmem((group, lists), BF),
            vmem((lists, 2 * hid), F32),
            vmem((lists, hid), F32),
            vmem((lists, 2 * hid), BF),
            vmem((lists, hid), BF),
            vmem((nc, cycle - 1, 2, cap, cw), BF),
            vmem((nc, cycle, 2, cap, cw), BF),
            vmem((cycle, 2, 8, cap), F32),
            vmem((cycle - 1, 8, cap), F32),
            vmem((nc, 2, own, cw), F32),
            vmem((nc, 2, own, cw), BF),
            vmem((nc, 2, own, cw), BF),
            vmem((nc, 2, own, cw), BF),
            vmem((nc, cw, 2 * hid), BF),
            vmem((nc, hid, cw), BF),
            dma((2, nc)), dma((2,)), dma((nc,)), dma,
            dma((2, nc)), dma((2, nc)), dma, dma,
            dma((2, nc)), dma((2, nc)), dma((2,)), dma((2,)),
            dma((2, nc)), dma((2, nc)), dma((cycle, 2)), dma((cycle, 2)),
            dma((nc,)), dma((nc,)),
            dma((2, nc)), dma((2, nc)), dma((nc,)),
        ],
        compiler_params=pltpu.CompilerParams(
            collective_id=0, has_side_effects=True, vmem_limit_bytes=60 * 1024 * 1024
        ),
        name="routed_experts",
    )(tokens, cotangent, padded, slot_rows, w_gate, w_up, w_down)
    mixed, in_grad, gates, d_gate, d_up, d_down = outs
    return mixed, in_grad, gates[:, :cycle], d_gate, d_up, d_down


def solution(mesh):
    in_specs = (
        P(("blk", "dp"), None),
        P(("blk", "dp"), None),
        P(("blk", "dp"), None),
        P("blk", None),
        P("blk", None, "dp"),
        P("blk", None, "dp"),
        P("blk", "dp", None),
    )
    out_specs = (
        P(("blk", "dp"), None),
        P(("blk", "dp"), None),
        P(("blk", "dp"), None),
        P("blk", None, "dp"),
        P("blk", None, "dp"),
        P("blk", "dp", None),
    )
    return jax.shard_map(
        on_device, mesh=mesh, in_specs=in_specs, out_specs=out_specs, check_vma=False
    )
```

time: 201 us -> 146 us (0.73)
  Pallas kernels: 0 us -> 134 us
  waiting for transfers between devices: 102 us -> 0 us
  starting transfers between devices: 49.6 us -> 0 us
  matrix products: 25.4 us -> 0 us
  between operations: 14.3 us -> 0.66 us
  local copies, waits for them, and re-layouts: 1 us -> 11.3 us
  blocking collectives: 5.47 us -> 0 us
  other arithmetic: 3.09 us -> 0 us
    pallas_call x0 -> x1, Pallas kernels: none -> 134 us  [on_device(): pl.pallas_call(body, out_shape=(jax.ShapeDtypeStruct((own, width), BF), j...]
    ppermute x15 -> x0, waiting for transfers between devices: 53.9 us -> none  [the longest x3 26.9 us: summed(): arrived = lax.ppermute(other.astype(kind), 'dp', [(0, 1), (1, 0)])]
    ppermute x15 -> x0, starting transfers between devices: 49.5 us -> none  [the longest x12 41.3 us: shifted(): return lax.ppermute(value, axis, pairs)]
    all_gather x2 -> x0, waiting for transfers between devices: 46.8 us -> none  [the longest x1 26.1 us: on_device(): group_dy = lax.all_gather(cotangent, 'dp', axis=0, tiled=True)]
    dot_general x14 -> x0, matrix products: 25.4 us -> none  [the longest x1 3.54 us: on_device(): jnp.einsum('cd,ch->dh', x, pgg, preferred_element_type=F32).astype(BF)]
    unnamed x11 -> x15, local copies, waits for them, and re-layouts: 0.12 us -> 10.6 us
    all_gather x1 -> x0, blocking collectives: 5.47 us -> none  [on_device(): group_gate = lax.all_gather(gate_probs, 'dp', axis=0, tiled=True)]
    convert_element_type x3 -> x0, other arithmetic: 2.11 us -> none  [the longest x1 1.05 us: on_device(): summed(input_grad, BF).astype(BF)]
  transfers between devices with their start and end apart: 17 -> 0, of which waited for: 8 -> 0; matrix products, arithmetic and copies ran while one was open for 13% -> 0% of each run, Pallas kernels for 0% -> 0%
where the time goes in v2:
time: 146 us
  Pallas kernels  134 us (92%)
  local copies, waits for them, and re-layouts  11.3 us (8%)
    pallas_call x1, Pallas kernels, on_device(): pl.pallas_call(body, out_shape=(jax.ShapeDtypeStruct((own, width), BF), j...  134 us
    unnamed x15, local copies, waits for them, and re-layouts  10.6 us

profile of v2, /device:TPU:1, one launch (start us, length us, event | category | flops | bytes accessed | tf_op | source)
XLA Modules:
  0.0 146.2 jit_solution(10144402288012044237)
XLA Ops:
  0.6 0.8 copy.13
  1.5 0.6 pad.4.refs_2_
  2.1 134.3 %routed_experts.1 = (bf16[192,2048]{1,0:T(8,128)(2,1)}, bf16[192,2048]{1,0:T(8,128)(2,1)}, f32[192,128]{1,0:T(8,128)}, bf16[1,2048,384]{2,1,0:T(8,128)(2,1)}, bf...) custom-call(bf16[192,2048]{1,0:T(8,128)(2,1)} %refs_0_.1, bf16[192,2048]{1,0:T(8,128)(2,1)} %refs_1_.1, ...), custom_call_target="tpu_custom_call" | custom-call | tf_op jit(solution)/shard_map/routed_experts/pallas_call | solution.py:312
  136.4 0.0 copy-start.3
  136.4 1.6 %copy.14 = f32[192,3]{0,1:T(4,128)} copy(f32[192,3]{1,0:T(8,128)} %bitcast.1) | data formatting | bytes 4608
  138.0 0.0 copy-start.2
  138.0 2.2 %copy.20 = bf16[192,2048]{1,0:T(8,128)(2,1)} copy(bf16[192,2048]{1,0:T(8,128)(2,1)} %get-tuple-element.30) | data formatting | bytes 1572864
  140.2 0.0 copy-done.3
  140.2 0.9 copy.21
  141.1 0.0 copy-done.2
  141.1 0.0 copy-start.1
  141.1 1.1 copy.22
  142.3 0.8 copy-done.1
  143.1 0.0 copy-start
  143.1 1.1 copy.23
  144.2 0.8 copy-done
  145.1 1.1 copy.24
Async XLA Ops:
  136.4 3.9 %copy-start.3 = (bf16[192,2048]{1,0:T(8,128)(2,1)S(1)}, bf16[192,2048]{1,0:T(8,128)(2,1)}, u32[]{:S(2)}) copy-start(bf16[192,2048]{1,0:T(8,128)(2,1)} %get-tuple-element.31) | copy-start | bytes 2359300
  138.0 3.1 %copy-start.2 = (bf16[1,2048,384]{2,1,0:T(8,128)(2,1)S(1)}, bf16[1,2048,384]{2,1,0:T(8,128)(2,1)}, u32[]{:S(2)}) copy-start(bf16[1,2048,384]{2,1,0:T(8,128)(2,1)} %get-tuple-element.33) | copy-start | bytes 4718596
  141.1 2.0 %copy-start.1 = (bf16[1,2048,384]{2,1,0:T(8,128)(2,1)S(1)}, bf16[1,2048,384]{2,1,0:T(8,128)(2,1)}, u32[]{:S(2)}) copy-start(bf16[1,2048,384]{2,1,0:T(8,128)(2,1)} %get-tuple-element.34) | copy-start | bytes 4718596
  143.1 2.0 %copy-start = (bf16[1,384,2048]{2,1,0:T(8,128)(2,1)S(1)}, bf16[1,384,2048]{2,1,0:T(8,128)(2,1)}, u32[]{:S(2)}) copy-start(bf16[1,384,2048]{2,1,0:T(8,128)(2,1)} %get-tuple-element.35) | copy-start | bytes 4718596

commit v3 on v2

--- a/solution.py
+++ b/solution.py
@@ -9,6 +9,9 @@
 F32 = jnp.float32
 MESH = pl.DeviceIdType.MESH
 CHUNKS = 8
+AHEAD = 8
+LAG = 2
+PARTS = 2
 
 
 def dot(a, b, ca=1, cb=0):
@@ -35,13 +38,18 @@
     def up(s):
         return lax.rem(b + s, blocks)
 
-    def down_dev(s, c):
+    def relayed(c):
+        return lax.rem(lax.div(c, 2), 2)
+
+    def down_route(s, c):
         cross = 1 - lax.div(x8 + 8 - s, 8)
-        return (down(s), lax.rem(h + cross * lax.rem(c, 2), 2))
-
-    def up_dev(s, c):
+        relay = cross * (relayed(c))
+        return (down(s + relay * (8 - s)), lax.rem(h + cross * lax.rem(c + s, 2), 2)), s + 2 * relay
+
+    def up_route(s, c):
         cross = lax.div(x8 + s, 8)
-        return (up(s), lax.rem(h + cross * lax.rem(c, 2), 2))
+        relay = cross * (lax.div(c, nc // 2))
+        return (up(s + relay * (8 - s)), lax.rem(h + cross * lax.rem(c + s, 2), 2)), s + 2 * relay
 
     def cols(c):
         return pl.ds(pl.multiple_of(c * cw, cw), cw)
@@ -55,14 +63,56 @@
             device_id=peer, device_id_type=MESH)
 
     def send_x(s, c):
-        return pltpu.make_async_remote_copy(
-            S.at[c, s - 1], E.at[c, s], xf_s.at[s - 1, c], xf_r.at[s - 1, c],
-            device_id=down_dev(s, c), device_id_type=MESH)
+        device, slot = down_route(s, c)
+        return pltpu.make_async_remote_copy(
+            S.at[c, s - 1], E.at[c, slot], xf_s.at[s - 1, c], xf_r.at[slot - 1, c],
+            device_id=device, device_id_type=MESH)
+
+    def take_x(slot, c):
+        return pltpu.make_async_remote_copy(
+            S.at[c, 0], E.at[c, slot], xf_s.at[0, c], xf_r.at[slot - 1, c], device_id=peer, device_id_type=MESH)
+
+    def relay_x(s, c):
+        return pltpu.make_async_remote_copy(
+            E.at[c, s + 2], E.at[c, s], xf_s.at[s + 1, c], xf_r.at[s - 1, c],
+            device_id=(lax.rem(b + 8 - s, blocks), h), device_id_type=MESH)
 
     def send_back(s, c):
-        return pltpu.make_async_remote_copy(
-            R.at[c, s - 1], RR.at[c, s], xr_s.at[s - 1, c], xr_r.at[s - 1, c],
-            device_id=up_dev(s, c), device_id_type=MESH)
+        device, slot = up_route(s, c)
+        return pltpu.make_async_remote_copy(
+            R.at[c, s - 1], RR.at[c, slot], xr_s.at[s - 1, c], xr_r.at[slot - 1, c],
+            device_id=device, device_id_type=MESH)
+
+    def take_back(slot, c):
+        return pltpu.make_async_remote_copy(
+            R.at[c, 0], RR.at[c, slot], xr_s.at[0, c], xr_r.at[slot - 1, c], device_id=peer, device_id_type=MESH)
+
+    def relay_back(s, c):
+        return pltpu.make_async_remote_copy(
+            RR.at[c, s + 2], RR.at[c, s], xr_s.at[s + 1, c], xr_r.at[s - 1, c],
+            device_id=(lax.rem(b + blocks - 8 + s, blocks), h), device_id_type=MESH)
+
+    def relays_x(c, act):
+        for s in (2, 1):
+
+            @pl.when((1 - lax.div(x8 + 8 - s, 8)) * (relayed(c)) == 1)
+            def _():
+                act(s, c)
+
+    def relays_back(c, act):
+        for s in (2, 1):
+
+            @pl.when(lax.div(x8 + s, 8) * (lax.div(c, nc // 2)) == 1)
+            def _():
+                act(s, c)
+
+    def pass_x(s, c):
+        take_x(s + 2, c).wait_recv()
+        relay_x(s, c).start()
+
+    def pass_back(s, c):
+        take_back(s + 2, c).wait_recv()
+        relay_back(s, c).start()
 
     def send_sum(c):
         return pltpu.make_async_remote_copy(
@@ -70,7 +120,7 @@
 
     def send_gate():
         return pltpu.make_async_remote_copy(
-            gate, G.at[pl.ds(own, own)], yg_s, yg_r, device_id=peer, device_id_type=MESH)
+            gate, G.at[1], yg_s, yg_r, device_id=peer, device_id_type=MESH)
 
     def send_list_gate(s):
         return pltpu.make_async_remote_copy(
@@ -86,10 +136,10 @@
     routes = [(0, 1), (1, 0), (1, 1), (2, 0), (2, 1)]
 
     bar = pltpu.get_barrier_semaphore()
-    near = [peer] + [(f(s), d) for f in (down, up) for s in (1, 2) for d in (h, 1 - h)]
+    near = [peer] + [(f(s), d) for f in (down, up) for s in (1, 2, 8) for d in (h, 1 - h)]
     for device in near:
         pl.semaphore_signal(bar, inc=1, device_id=device, device_id_type=MESH)
-    load_gate = pltpu.make_async_copy(gate, G.at[pl.ds(0, own)], ld_g)
+    load_gate = pltpu.make_async_copy(gate, G.at[0], ld_g)
     load_gate.start()
 
     def begin(c, _):
@@ -106,7 +156,7 @@
         send_y(1, c).start()
         return 0
 
-    lax.fori_loop(0, nc, cross, 0)
+    lax.fori_loop(0, 2, cross, 0)
     load_wg = pltpu.make_async_copy(w_g.at[0], WGU.at[:, pl.ds(0, hid)], ld_w.at[0])
     load_wu = pltpu.make_async_copy(w_u.at[0], WGU.at[:, pl.ds(hid, hid)], ld_w.at[1])
     load_wg.start()
@@ -136,7 +186,9 @@
     load_gate.wait()
     send_gate().wait_recv()
     for s in (2, 1, 0):
-        picked = dot(PICK[s * cap : (s + 1) * cap, :], G[...]).astype(BF)
+        span = slice(s * cap, (s + 1) * cap)
+        row = dot(G[0], PUT[0:own, span]) + dot(G[1], PUT[own : 2 * own, span])
+        picked = jnp.broadcast_to(row[s : s + 1, :], (cap, cap)).T.astype(BF)
         if s:
             GS[s - 1] = picked
             send_list_gate(s).start()
@@ -146,11 +198,11 @@
     load_wu.wait()
 
     def project(c):
-        send_x(1, c).wait_recv()
-        send_x(2, c).wait_recv()
+        take_x(1, c).wait_recv()
+        take_x(2, c).wait_recv()
         load_wd(c).wait()
-        x = E[c, :, 0].reshape(3 * cap, cw)
-        dy = E[c, :, 1].reshape(3 * cap, cw)
+        x = E[c, 0:3, 0].reshape(3 * cap, cw)
+        dy = E[c, 0:3, 1].reshape(3 * cap, cw)
         PRE[...] += dot(x, WGU[pl.ds(pl.multiple_of(c * cw, cw), cw), :])
         BACK[...] += dot(dy, WD[c], 1, 1)
 
@@ -166,13 +218,23 @@
         send_x(2, c).start()
         send_x(1, c).start()
 
+        @pl.when(c < nc - 2)
+        def _():
+            cross(c + 2, 0)
+
         @pl.when(c > 0)
         def _():
-            project(c - 1)
+            relays_x(c - 1, pass_x)
+
+        @pl.when(c > 1)
+        def _():
+            project(c - 2)
 
         return 0
 
     lax.fori_loop(0, nc, forward, 0)
+    relays_x(nc - 1, pass_x)
+    project(nc - 2)
     project(nc - 1)
     send_list_gate(1).wait_recv()
     send_list_gate(2).wait_recv()
@@ -208,7 +270,7 @@
         send_back(1, c).start()
         return 0
 
-    lax.fori_loop(0, nc, results, 0)
+    lax.fori_loop(0, AHEAD, results, 0)
     for s, rel in routes:
         send_gate_grad(s, rel).start()
 
@@ -219,17 +281,14 @@
     def store_d(c):
         return pltpu.make_async_copy(DD.at[c], o_dd.at[0, :, cols(c)], st_d.at[c])
 
-    def weight_grads(c, _):
-        x = E[c, :, 0].reshape(3 * cap, cw)
-        dy = E[c, :, 1].reshape(3 * cap, cw)
+    def weight_grads(c):
+        x = E[c, 0:3, 0].reshape(3 * cap, cw)
+        dy = E[c, 0:3, 1].reshape(3 * cap, cw)
         DGU[c] = dot(x, PGU[...], 0, 0).astype(BF)
         DD[c] = dot(HW[...], dy, 0, 0).astype(BF)
         store_w(0, c).start()
         store_w(1, c).start()
         store_d(c).start()
-        return 0
-
-    lax.fori_loop(0, nc, weight_grads, 0)
 
     def store_out(k, c):
         return pltpu.make_async_copy(OUT.at[c, k], (o_mix, o_in)[k].at[:, cols(c)], st_o.at[k, c])
@@ -241,18 +300,25 @@
             store_out(k, c).start()
 
     def collect(c, _):
-        send_back(1, c).wait_recv()
-        send_back(2, c).wait_recv()
+        @pl.when(c < nc - AHEAD)
+        def _():
+            results(c + AHEAD, 0)
+
+        relays_back(c, pass_back)
+        take_back(1, c).wait_recv()
+        take_back(2, c).wait_recv()
         for k in range(2):
-            rows = RR[c, :, k].reshape(3 * cap, cw)
+            rows = RR[c, 0:3, k].reshape(3 * cap, cw)
             total = dot(PUT[...], rows)
             YS[c, k] = total[own : 2 * own].astype(BF)
             OWN[c, k] = total[0:own]
         send_sum(c).start()
 
-        @pl.when(c > 1)
+        weight_grads(c)
+
+        @pl.when(c >= LAG)
         def _():
-            finish(c - 2)
+            finish(c - LAG)
 
         return 0
 
@@ -267,10 +333,13 @@
         named = PUT[0:own, s * cap : (s + 1) * cap].astype(F32)
         column = jnp.sum(jnp.where(named > 0.5, jnp.broadcast_to(row, (own, cap)), 0.0), axis=1, keepdims=True)
         grads = jnp.where(lane == s, column, grads)
-    o_gate[...] = grads
-
-    finish(nc - 2)
-    finish(nc - 1)
+    o_gate[...] = grads.T[0:3, :]
+
+    def finish_last(c, _):
+        finish(c)
+        return 0
+
+    lax.fori_loop(nc - LAG, nc, finish_last, 0)
 
     send_gate().wait_send()
     for s in (1, 2):
@@ -288,9 +357,53 @@
             send_back(s, c).wait_send()
         send_sum(c).wait_send()
         store_d(c).wait()
+        relays_x(c, lambda s, c: relay_x(s, c).wait_send())
+        relays_back(c, lambda s, c: relay_back(s, c).wait_send())
         return 0
 
     lax.fori_loop(0, nc, drain, 0)
+
+
+def hand_out(arrays):
+    big = [i for i, a in enumerate(arrays) if a.size > 4096]
+
+    def body(*refs):
+        n = len(arrays)
+        src, dst, hold = refs[:n], refs[n : 2 * n], refs[2 * n : 2 * n + len(big)]
+        rd, wr = refs[-2], refs[-1]
+        pieces = []
+        for j, i in enumerate(big):
+            ref = (src[i], dst[i], hold[j])
+            if len(ref[0].shape) == 3:
+                ref = (ref[0].at[0], ref[1].at[0], ref[2].at[0])
+            rows = ref[0].shape[0] // PARTS
+            for p in range(PARTS):
+                at = pl.ds(p * rows, rows)
+                read = pltpu.make_async_copy(ref[0].at[at], ref[2].at[at], rd.at[j, p])
+                write = pltpu.make_async_copy(ref[2].at[at], ref[1].at[at], wr.at[j, p])
+                pieces.append((read, write))
+        for read, _ in pieces:
+            read.start()
+        for i in range(n):
+            if i not in big:
+                dst[i][...] = src[i][...]
+        for read, write in pieces:
+            read.wait()
+            write.start()
+        for _, write in pieces:
+            write.wait()
+
+    specs = [pl.BlockSpec(memory_space=pl.ANY if i in big else pltpu.VMEM) for i in range(len(arrays))]
+    return pl.pallas_call(
+        body,
+        out_shape=tuple(jax.ShapeDtypeStruct(a.shape, a.dtype) for a in arrays),
+        in_specs=specs,
+        out_specs=tuple(specs),
+        scratch_shapes=[pltpu.VMEM(arrays[i].shape, arrays[i].dtype) for i in big]
+        + [pltpu.SemaphoreType.DMA((len(big), PARTS))] * 2,
+        compiler_params=pltpu.CompilerParams(vmem_limit_bytes=60 * 1024 * 1024),
+        name="hand_out",
+    )(*arrays)
 
 
 def on_device(tokens, cotangent, gate_probs, slot_rows, w_gate, w_up, w_down):
@@ -300,7 +413,7 @@
     nc, cw = CHUNKS, width // CHUNKS
     group, lists = 2 * own, cycle * cap
     blocks = lax.axis_size("blk")
-    padded = jnp.pad(gate_probs, ((0, 0), (0, cap - cycle)))
+    hops = 2 * (cycle - 1)
     dma = pltpu.SemaphoreType.DMA
     vmem = pltpu.VMEM
     any_space = pl.BlockSpec(memory_space=pl.ANY)
@@ -314,7 +427,7 @@
         out_shape=(
             jax.ShapeDtypeStruct((own, width), BF),
             jax.ShapeDtypeStruct((own, width), BF),
-            jax.ShapeDtypeStruct((own, cap), F32),
+            jax.ShapeDtypeStruct((cycle, own), F32),
             jax.ShapeDtypeStruct(w_gate.shape, BF),
             jax.ShapeDtypeStruct(w_up.shape, BF),
             jax.ShapeDtypeStruct(w_down.shape, BF),
@@ -323,9 +436,9 @@
         out_specs=(any_space, any_space, in_vmem, any_space, any_space, any_space),
         scratch_shapes=[
             vmem((nc, 2, group, cw), BF),
-            vmem((nc, cycle, 2, cap, cw), BF),
+            vmem((nc, 1 + hops, 2, cap, cw), BF),
             vmem((nc, cycle - 1, 2, cap, cw), BF),
-            vmem((group, cap), BF),
+            vmem((2, cycle, own), BF),
             vmem((cycle, cap, cap), BF),
             vmem((cycle - 1, cap, cap), BF),
             vmem((width, 2 * hid), BF),
@@ -337,7 +450,7 @@
             vmem((lists, 2 * hid), BF),
             vmem((lists, hid), BF),
             vmem((nc, cycle - 1, 2, cap, cw), BF),
-            vmem((nc, cycle, 2, cap, cw), BF),
+            vmem((nc, 1 + hops, 2, cap, cw), BF),
             vmem((cycle, 2, 8, cap), F32),
             vmem((cycle - 1, 8, cap), F32),
             vmem((nc, 2, own, cw), F32),
@@ -348,8 +461,8 @@
             vmem((nc, hid, cw), BF),
             dma((2, nc)), dma((2,)), dma((nc,)), dma,
             dma((2, nc)), dma((2, nc)), dma, dma,
-            dma((2, nc)), dma((2, nc)), dma((2,)), dma((2,)),
-            dma((2, nc)), dma((2, nc)), dma((cycle, 2)), dma((cycle, 2)),
+            dma((hops, nc)), dma((hops, nc)), dma((2,)), dma((2,)),
+            dma((hops, nc)), dma((hops, nc)), dma((cycle, 2)), dma((cycle, 2)),
             dma((nc,)), dma((nc,)),
             dma((2, nc)), dma((2, nc)), dma((nc,)),
         ],
@@ -357,9 +470,9 @@
             collective_id=0, has_side_effects=True, vmem_limit_bytes=60 * 1024 * 1024
         ),
         name="routed_experts",
-    )(tokens, cotangent, padded, slot_rows, w_gate, w_up, w_down)
-    mixed, in_grad, gates, d_gate, d_up, d_down = outs
-    return mixed, in_grad, gates[:, :cycle], d_gate, d_up, d_down
+    )(tokens, cotangent, gate_probs.T, slot_rows, w_gate, w_up, w_down)
+    mixed, in_grad, gates, d_gate, d_up, d_down = hand_out(outs)
+    return mixed, in_grad, gates.T, d_gate, d_up, d_down
 
 
 def solution(mesh):

time: 146 us -> 132 us (0.904)
  the two profiles are of different devices: /device:TPU:1 before, /device:TPU:6 now
where the time goes in v3:
time: 132 us
  Pallas kernels  131 us (99%)
    pallas_call x1, Pallas kernels, on_device(): pl.pallas_call(body, out_shape=(jax.ShapeDtypeStruct((own, width), BF), j...  125 us
    pallas_call x1, Pallas kernels, hand_out(): pl.pallas_call(body, out_shape=tuple((jax.ShapeDtypeStruct(a.shape, a.dty...  6.54 us

profile of v3, /device:TPU:6, one launch (start us, length us, event | category | flops | bytes accessed | tf_op | source)
XLA Modules:
  0.0 132.0 jit_solution(785677758755133499)
XLA Ops:
  0.6 124.8 %routed_experts.1 = (bf16[192,2048]{1,0:T(8,128)(2,1)}, bf16[192,2048]{1,0:T(8,128)(2,1)}, f32[3,192]{1,0:T(4,128)}, bf16[1,2048,384]{2,1,0:T(8,128)(2,1)}, bf16...) custom-call(bf16[192,2048]{1,0:T(8,128)(2,1)} %refs_0_.1, bf16[192,2048]{1,0:T(8,128)(2,1)} %refs_1_.1, ...), custom_call_target="tpu_custom_call" | custom-call | tf_op jit(solution)/shard_map/routed_experts/pallas_call | solution.py:425
  125.4 6.5 %hand_out.1 = (bf16[192,2048]{1,0:T(8,128)(2,1)}, bf16[192,2048]{1,0:T(8,128)(2,1)}, f32[3,192]{1,0:T(4,128)}, bf16[1,2048,384]{2,1,0:T(8,128)(2,1)}, bf16[1,204...) custom-call(bf16[192,2048]{1,0:T(8,128)(2,1)} %get-tuple-element.18.refs_0_, ...), custom_call_target="tpu_custom_call" | custom-call | tf_op jit(solution)/shard_map/hand_out/pallas_call | solution.py:397

commit v4 on v3

--- a/solution.py
+++ b/solution.py
@@ -11,7 +11,8 @@
 CHUNKS = 8
 AHEAD = 8
 LAG = 2
-PARTS = 2
+RELAY_LAG = 2
+PROJECT_LAG = 4
 
 
 def dot(a, b, ca=1, cb=0):
@@ -38,18 +39,25 @@
     def up(s):
         return lax.rem(b + s, blocks)
 
-    def relayed(c):
-        return lax.rem(lax.div(c, 2), 2)
+    def turn_x(c):
+        return lax.rem(c, 4)
+
+    def turn_back(c):
+        return lax.div(c, nc // 4) + lax.div(c, nc // 2) - 2 * lax.div(c, 3 * (nc // 4))
 
     def down_route(s, c):
         cross = 1 - lax.div(x8 + 8 - s, 8)
-        relay = cross * (relayed(c))
-        return (down(s + relay * (8 - s)), lax.rem(h + cross * lax.rem(c + s, 2), 2)), s + 2 * relay
+        turn = turn_x(c)
+        relay = cross * lax.div(turn + 3, 4)
+        plane = lax.rem(h + cross * lax.rem(lax.div(c, 4) + s, 2), 2)
+        return (down(s + relay * (10 - 2 * turn - s)), plane), s + 2 * relay
 
     def up_route(s, c):
         cross = lax.div(x8 + s, 8)
-        relay = cross * (lax.div(c, nc // 2))
-        return (up(s + relay * (8 - s)), lax.rem(h + cross * lax.rem(c + s, 2), 2)), s + 2 * relay
+        turn = turn_back(c)
+        relay = cross * lax.div(turn + 3, 4)
+        plane = lax.rem(h + cross * lax.rem(c + s, 2), 2)
+        return (up(s + relay * (10 - 2 * turn - s)), plane), s + 2 * relay
 
     def cols(c):
         return pl.ds(pl.multiple_of(c * cw, cw), cw)
@@ -75,7 +83,7 @@
     def relay_x(s, c):
         return pltpu.make_async_remote_copy(
             E.at[c, s + 2], E.at[c, s], xf_s.at[s + 1, c], xf_r.at[s - 1, c],
-            device_id=(lax.rem(b + 8 - s, blocks), h), device_id_type=MESH)
+            device_id=(lax.rem(b + blocks + 10 - 2 * turn_x(c) - s, blocks), h), device_id_type=MESH)
 
     def send_back(s, c):
         device, slot = up_route(s, c)
@@ -90,19 +98,23 @@
     def relay_back(s, c):
         return pltpu.make_async_remote_copy(
             RR.at[c, s + 2], RR.at[c, s], xr_s.at[s + 1, c], xr_r.at[s - 1, c],
-            device_id=(lax.rem(b + blocks - 8 + s, blocks), h), device_id_type=MESH)
+            device_id=(lax.rem(b + blocks - 10 + 2 * turn_back(c) + s, blocks), h), device_id_type=MESH)
 
     def relays_x(c, act):
         for s in (2, 1):
 
-            @pl.when((1 - lax.div(x8 + 8 - s, 8)) * (relayed(c)) == 1)
+            core = x8 - 2 * (turn_x(c) - 1)
+
+            @pl.when((turn_x(c) > 0) & (core >= 0) & (core < s))
             def _():
                 act(s, c)
 
     def relays_back(c, act):
         for s in (2, 1):
 
-            @pl.when(lax.div(x8 + s, 8) * (lax.div(c, nc // 2)) == 1)
+            core = x8 - 8 + 2 * turn_back(c)
+
+            @pl.when((turn_back(c) > 0) & (core <= 1) & (core >= 2 - s))
             def _():
                 act(s, c)
 
@@ -136,7 +148,7 @@
     routes = [(0, 1), (1, 0), (1, 1), (2, 0), (2, 1)]
 
     bar = pltpu.get_barrier_semaphore()
-    near = [peer] + [(f(s), d) for f in (down, up) for s in (1, 2, 8) for d in (h, 1 - h)]
+    near = [peer] + [(f(s), d) for f in (down, up) for s in (1, 2, 4, 6, 8) for d in (h, 1 - h)]
     for device in near:
         pl.semaphore_signal(bar, inc=1, device_id=device, device_id_type=MESH)
     load_gate = pltpu.make_async_copy(gate, G.at[0], ld_g)
@@ -222,20 +234,25 @@
         def _():
             cross(c + 2, 0)
 
-        @pl.when(c > 0)
+        @pl.when(c >= RELAY_LAG)
         def _():
-            relays_x(c - 1, pass_x)
-
-        @pl.when(c > 1)
+            relays_x(c - RELAY_LAG, pass_x)
+
+        @pl.when(c >= PROJECT_LAG)
         def _():
-            project(c - 2)
+            project(c - PROJECT_LAG)
 
         return 0
 
     lax.fori_loop(0, nc, forward, 0)
-    relays_x(nc - 1, pass_x)
-    project(nc - 2)
-    project(nc - 1)
+    for c in range(nc - RELAY_LAG, nc):
+        relays_x(c, pass_x)
+
+    def project_last(c, _):
+        project(c)
+        return 0
+
+    lax.fori_loop(nc - PROJECT_LAG, nc, project_last, 0)
     send_list_gate(1).wait_recv()
     send_list_gate(2).wait_recv()
 
@@ -369,29 +386,16 @@
 
     def body(*refs):
         n = len(arrays)
-        src, dst, hold = refs[:n], refs[n : 2 * n], refs[2 * n : 2 * n + len(big)]
-        rd, wr = refs[-2], refs[-1]
-        pieces = []
-        for j, i in enumerate(big):
-            ref = (src[i], dst[i], hold[j])
-            if len(ref[0].shape) == 3:
-                ref = (ref[0].at[0], ref[1].at[0], ref[2].at[0])
-            rows = ref[0].shape[0] // PARTS
-            for p in range(PARTS):
-                at = pl.ds(p * rows, rows)
-                read = pltpu.make_async_copy(ref[0].at[at], ref[2].at[at], rd.at[j, p])
-                write = pltpu.make_async_copy(ref[2].at[at], ref[1].at[at], wr.at[j, p])
-                pieces.append((read, write))
-        for read, _ in pieces:
-            read.start()
+        src, dst = refs[:n], refs[n : 2 * n]
+        wr = refs[-1]
+        copies = [pltpu.make_async_copy(src[i], dst[i], wr.at[j]) for j, i in enumerate(big)]
+        for copy in copies:
+            copy.start()
         for i in range(n):
             if i not in big:
                 dst[i][...] = src[i][...]
-        for read, write in pieces:
-            read.wait()
-            write.start()
-        for _, write in pieces:
-            write.wait()
+        for copy in copies:
+            copy.wait()
 
     specs = [pl.BlockSpec(memory_space=pl.ANY if i in big else pltpu.VMEM) for i in range(len(arrays))]
     return pl.pallas_call(
@@ -399,9 +403,8 @@
         out_shape=tuple(jax.ShapeDtypeStruct(a.shape, a.dtype) for a in arrays),
         in_specs=specs,
         out_specs=tuple(specs),
-        scratch_shapes=[pltpu.VMEM(arrays[i].shape, arrays[i].dtype) for i in big]
-        + [pltpu.SemaphoreType.DMA((len(big), PARTS))] * 2,
-        compiler_params=pltpu.CompilerParams(vmem_limit_bytes=60 * 1024 * 1024),
+        scratch_shapes=[pltpu.SemaphoreType.DMA((len(big),))],
+        compiler_params=pltpu.CompilerParams(vmem_limit_bytes=1024 * 1024),
         name="hand_out",
     )(*arrays)
 
@@ -467,7 +470,7 @@
             dma((2, nc)), dma((2, nc)), dma((nc,)),
         ],
         compiler_params=pltpu.CompilerParams(
-            collective_id=0, has_side_effects=True, vmem_limit_bytes=60 * 1024 * 1024
+            collective_id=0, has_side_effects=True, vmem_limit_bytes=46 * 1024 * 1024
         ),
         name="routed_experts",
     )(tokens, cotangent, gate_probs.T, slot_rows, w_gate, w_up, w_down)

time: 132 us -> 128 us (0.970)
  the two profiles are of different devices: /device:TPU:6 before, /device:TPU:1 now
where the time goes in v4:
time: 128 us
  Pallas kernels  124 us (97%)
  local copies, waits for them, and re-layouts  3.62 us (3%)
    pallas_call x1, Pallas kernels, on_device(): pl.pallas_call(body, out_shape=(jax.ShapeDtypeStruct((own, width), BF), j...  120 us
    unnamed x8, local copies, waits for them, and re-layouts  3.62 us
    pallas_call x1, Pallas kernels, hand_out(): pl.pallas_call(body, out_shape=tuple((jax.ShapeDtypeStruct(a.shape, a.dty...  3.33 us

profile of v4, /device:TPU:1, one launch (start us, length us, event | category | flops | bytes accessed | tf_op | source)
XLA Modules:
  0.0 128.0 jit_solution(7968488042142575339)
XLA Ops:
  0.6 0.0 copy-start
  0.6 1.1 copy-done
  1.8 0.0 copy-start.1
  1.8 1.1 copy-done.1
  2.9 0.0 copy-start.2
  2.9 0.7 copy-done.2
  3.6 0.0 copy-start.3
  3.6 0.7 copy-done.3
  4.3 120.4 %routed_experts.1 = (bf16[192,2048]{1,0:T(8,128)(2,1)S(1)}, bf16[192,2048]{1,0:T(8,128)(2,1)S(1)}, f32[3,192]{1,0:T(4,128)S(1)}, bf16[1,2048,384]{2,1,0:T(8,128)...) custom-call(bf16[192,2048]{1,0:T(8,128)(2,1)S(1)} %copy-done, ...), custom_call_target="tpu_custom_call" | custom-call | tf_op jit(solution)/shard_map/routed_experts/pallas_call | solution.py:428
  124.6 3.3 %hand_out.1 = (bf16[192,2048]{1,0:T(8,128)(2,1)}, bf16[192,2048]{1,0:T(8,128)(2,1)}, f32[3,192]{1,0:T(4,128)}, bf16[1,2048,384]{2,1,0:T(8,128)(2,1)}, bf16[1,204...) custom-call(bf16[192,2048]{1,0:T(8,128)(2,1)S(1)} %get-tuple-element.18.refs_0_, ...), custom_call_target="tpu_custom_call" | custom-call | tf_op jit(solution)/shard_map/hand_out/pallas_call | solution.py:401
Async XLA Ops:
  0.6 1.1 copy-start
  1.8 1.1 copy-start.1
  2.9 0.7 copy-start.2
  3.6 0.7 copy-start.3

commit v5 on v4

--- a/solution.py
+++ b/solution.py
@@ -421,6 +421,9 @@
     vmem = pltpu.VMEM
     any_space = pl.BlockSpec(memory_space=pl.ANY)
     in_vmem = pl.BlockSpec(memory_space=pltpu.VMEM)
+
+    def hold(a):
+        return pltpu.with_memory_space_constraint(a, pltpu.HBM)
 
     def body(*refs):
         kernel(blocks, *refs)
@@ -473,7 +476,7 @@
             collective_id=0, has_side_effects=True, vmem_limit_bytes=46 * 1024 * 1024
         ),
         name="routed_experts",
-    )(tokens, cotangent, gate_probs.T, slot_rows, w_gate, w_up, w_down)
+    )(hold(tokens), hold(cotangent), hold(gate_probs.T), slot_rows, hold(w_gate), hold(w_up), hold(w_down))
     mixed, in_grad, gates, d_gate, d_up, d_down = hand_out(outs)
     return mixed, in_grad, gates.T, d_gate, d_up, d_down
 

time: 128 us -> 125 us (0.977)
  local copies, waits for them, and re-layouts: 3.62 us -> 0.67 us
    unnamed x8 -> x2, local copies, waits for them, and re-layouts: 3.62 us -> 0.67 us
where the time goes in v5:
time: 125 us
  Pallas kernels  124 us (99%)
    pallas_call x1, Pallas kernels, on_device(): pl.pallas_call(body, out_shape=(jax.ShapeDtypeStruct((own, width), BF), j...  121 us
    pallas_call x1, Pallas kernels, hand_out(): pl.pallas_call(body, out_shape=tuple((jax.ShapeDtypeStruct(a.shape, a.dty...  3.33 us

profile of v5, /device:TPU:1, one launch (start us, length us, event | category | flops | bytes accessed | tf_op | source)
XLA Modules:
  0.0 125.4 jit_solution(3426010439179406371)
XLA Ops:
  0.6 0.0 copy-start
  0.6 0.7 copy-done
  1.3 120.7 %routed_experts.1 = (bf16[192,2048]{1,0:T(8,128)(2,1)S(1)}, bf16[192,2048]{1,0:T(8,128)(2,1)S(1)}, f32[3,192]{1,0:T(4,128)S(1)}, bf16[1,2048,384]{2,1,0:T(8,128)...) custom-call(bf16[192,2048]{1,0:T(8,128)(2,1)} %refs_0_.1, bf16[192,2048]{1,0:T(8,128)(2,1)} %refs_1_.1, ...), custom_call_target="tpu_custom_call" | custom-call | tf_op jit(solution)/shard_map/routed_experts/pallas_call | solution.py:431
  122.0 3.3 %hand_out.1 = (bf16[192,2048]{1,0:T(8,128)(2,1)}, bf16[192,2048]{1,0:T(8,128)(2,1)}, f32[3,192]{1,0:T(4,128)}, bf16[1,2048,384]{2,1,0:T(8,128)(2,1)}, bf16[1,204...) custom-call(bf16[192,2048]{1,0:T(8,128)(2,1)S(1)} %get-tuple-element.18.refs_0_, ...), custom_call_target="tpu_custom_call" | custom-call | tf_op jit(solution)/shard_map/hand_out/pallas_call | solution.py:401
Async XLA Ops:
  0.6 0.7 copy-start
